TPU v7x, 32 devices: a whole 2x2x4 slice. The times are simulated.
32 devices in a mesh: groups: 2 (over x), blk: 16 (over z, y, core).
Axes of the slice: x: 2, y: 2, z: 4, core: 2. Of those that a mesh axis runs over, the one named last changes fastest.
Arguments:
- item_rows: bfloat16 [16384, 1024], P(('groups', 'blk')), parts along dimension 0, may hold values from -6 to 6
- item_slot: int32 [16384], P('groups'), parts along dimension 0, may hold values from 0 to 8191, as said below
- w_up: bfloat16 [1024, 2048], replicated, may hold values from -0.1875 to 0.1875
- w_down: bfloat16 [2048, 1024], replicated, may hold values from -0.125 to 0.125
- events: bfloat16 [2048, 1024], P(('groups', 'blk')), parts along dimension 0, may hold values from -6 to 6
- w_query: bfloat16 [1024, 1024], replicated, may hold values from -0.1875 to 0.1875
- history_kv: bfloat16 [2048, 2, 1024], P(('groups', 'blk')), parts along dimension 0, may hold values from -6 to 6
- window_start: int32 [2048], P(('groups', 'blk')), parts along dimension 0, may hold values from 0 to 1023, as said below
- cand: int32 [2048, 16], P(('groups', 'blk')), parts along dimension 0, may hold values from 0 to 8191, as said below
- cand_count: int32 [2048], P(('groups', 'blk')), parts along dimension 0, may hold values from 1 to 16
Outputs:
- item_out: bfloat16 [16384, 1024], P(('groups', 'blk')), parts along dimension 0
- scores: float32 [2048, 16], P(('groups', 'blk')), parts along dimension 0
There are 2 independent parts, one for each index of `groups`. A program takes and returns all parts, laid end to end along the dimension named above; an argument that names none is the same for every part. Nothing has to cross between parts.
Inputs may be any that keep to these rules, and one draw needn't show every extreme that they name: A permutation of the item ids; item id m lies on the owner item_slot[m] // 512. `cand`: of the 1024 slots of one device, at most 128 name items of one owner; some owner is named by exactly 128 slots of every device. window_start[i] <= i and i - window_start[i] < 512; i - window_start[i] = 511 for some event.
All inputs are finite; a program needn't handle non-finite values.
Results may differ from a plain program's by a relative error of at most 0.0067.
Values may be sent and summed in bfloat16 or wider, within the bound.
No kernel may reach another device: no remote copies, remote signals or barrier semaphores. Data moves between devices by JAX's collectives and lax.ppermute only.
A program may use at most 128 MiB of HBM per device.

v0:
```python
import functools

import jax
import jax.numpy as jnp
from jax import lax
from jax.experimental import pallas as pl
from jax.experimental.pallas import tpu as pltpu
from jax.sharding import PartitionSpec as P


HEADS = 8
WIN = 512
PLANE = 4
LANES = 128
TILE = 512

VMEM_SPEC = pl.BlockSpec(memory_space=pltpu.VMEM)
HBM_SPEC = pl.BlockSpec(memory_space=pltpu.MemorySpace.HBM)
VMEM_LIMIT = 24 * 1024 * 1024
QUERY_GRANT = 66_400_000
MLP_GRANT = 62_000_000


def call(body, out_shape, args, scratch=(), flops=0, grant=None, first_out=None):
    size = sum(a.size * a.dtype.itemsize for a in args)
    out_specs = jax.tree.map(lambda _: VMEM_SPEC, out_shape)
    if first_out is not None:
        out_specs[0] = first_out
    return pl.pallas_call(
        body,
        out_shape=out_shape,
        in_specs=[HBM_SPEC if grant else VMEM_SPEC] * len(args),
        out_specs=out_specs,
        scratch_shapes=list(scratch),
        compiler_params=pltpu.CompilerParams(vmem_limit_bytes=grant or VMEM_LIMIT),
        cost_estimate=pl.CostEstimate(flops=flops, bytes_accessed=size, transcendentals=0),
    )(*args)


def in_plane(value, step):
    count = lax.axis_size("blk")
    pairs = [(s, (s // PLANE) * PLANE + ((s % PLANE) ^ step)) for s in range(count)]
    return lax.ppermute(value, "blk", pairs)


def forward(value, step):
    count = lax.axis_size("blk")
    return lax.ppermute(value, "blk", [(s, (s + step * PLANE) % count) for s in range(count)])


def swap(value, step):
    count = lax.axis_size("blk")
    return lax.ppermute(value, "blk", [(s, s ^ (step * PLANE)) for s in range(count)])


def my_place():
    index = lax.axis_index("blk")
    return index // PLANE, index % PLANE


def part_windows(part):
    column = my_place()[1]
    return [pl.ds(pl.multiple_of((column ^ step) * part, part), part) for step in range(PLANE)]


def copies_of(pairs, sems):
    return [
        pltpu.make_async_copy(source, target, sems.at[at])
        for at, (source, target) in enumerate(pairs)
    ]


def kv_pieces_kernel(kv_ref, *rest):
    outs, (key_buf, value_buf) = rest[:PLANE], rest[PLANE:]
    part = outs[0].shape[1] // 2
    windows = part_windows(part)
    key_buf[...] = kv_ref[:, 0, :]
    value_buf[...] = kv_ref[:, 1, :]
    for step in range(PLANE):
        outs[step][:, :part] = key_buf[:, windows[step]]
        outs[step][:, part:] = value_buf[:, windows[step]]


def query_kernel(event_hbm, weight_hbm, cand_hbm, table_hbm, start_hbm, *rest):
    query_outs, rest = rest[:PLANE], rest[PLANE:]
    event_ref, weight_ref, cand_ref, table_ref, start_ref, query_buf, sems = rest
    index = lax.axis_index("blk")
    hist_rows = event_ref.shape[0]
    part = query_outs[0].shape[1]
    windows = part_windows(part)
    copies = copies_of(
        [
            (cand_hbm, cand_ref),
            (table_hbm, table_ref),
            (start_hbm, start_ref),
            (event_hbm, event_ref),
            (weight_hbm, weight_ref),
        ],
        sems,
    )
    for copy in copies:
        copy.start()
    for copy in copies[:3]:
        copy.wait()
    ids = cand_ref[...]
    ids = jnp.concatenate([ids, ids], axis=1)
    table_row = ids // LANES
    table_lane = ids % LANES

    def look(row, found):
        values = jnp.broadcast_to(table_ref[pl.ds(row, 1), :], ids.shape)
        picked = jnp.take_along_axis(values, table_lane, axis=1, mode="promise_in_bounds")
        return jnp.where(table_row == row, picked, found)

    slot = lax.fori_loop(0, table_ref.shape[0], look, jnp.zeros_like(ids), unroll=8)
    first_half = lax.broadcasted_iota(jnp.int32, ids.shape, 1) < hist_rows
    slot_meta = jnp.where(first_half, slot // 256, slot % 256)
    starts = start_ref[...]
    starts = jnp.concatenate([starts, starts], axis=1)
    place = index * hist_rows + lax.broadcasted_iota(jnp.int32, starts.shape, 1) % hist_rows
    reach = index * hist_rows + hist_rows - WIN
    offset = place - jnp.maximum(starts, reach)
    offset = jnp.broadcast_to(offset, ids.shape)
    offset_meta = jnp.where(first_half, offset // 16, offset % 16)
    meta = jnp.concatenate([slot_meta, offset_meta], axis=1)
    meta = meta.astype(jnp.float32).astype(jnp.bfloat16)
    for copy in copies[3:]:
        copy.wait()
    query = jnp.dot(event_ref[...], weight_ref[...], preferred_element_type=jnp.float32)
    query_buf[...] = query.astype(jnp.bfloat16)
    for step in range(PLANE):
        query_outs[step][:hist_rows, :] = query_buf[:, windows[step]]
        query_outs[step][hist_rows:, :] = meta


def join_kernel(*refs):
    pieces, (all_ref, late_ref) = refs[:PLANE], refs[PLANE:]
    column = my_place()[1]
    rows = pieces[0].shape[0]
    for step in range(PLANE):
        all_ref[step * rows : (step + 1) * rows, :] = pieces[step][...]
    for block in range(1, PLANE):
        start = pl.multiple_of((column ^ block) * rows, rows)
        late_ref[(block - 1) * rows : block * rows, :] = all_ref[pl.ds(start, rows), :]


def collect_kernel(hist_rows, *refs):
    out_ref = refs[-1]
    slots = refs[0].shape[0] - hist_rows
    for step in range(PLANE):
        out_ref[step * slots : (step + 1) * slots, :] = refs[step][hist_rows:, :LANES]


def attend_kernel(hist_rows, shifts, *refs):
    queries, out_ref = refs[:PLANE], refs[-1]
    blocks = refs[PLANE:-1]
    plane, column = my_place()
    part = queries[0].shape[1]
    rows = PLANE * hist_rows
    head_size = out_ref.shape[1] * PLANE // HEADS
    heads = part // head_size
    scale = head_size**-0.5

    def positions(shape, axis, shift):
        at = lax.broadcasted_iota(jnp.int32, shape, axis)
        full = shape[axis] == rows
        block = (column ^ (at // hist_rows)) if full else 1 + at // hist_rows
        return ((plane - shift) * PLANE + block) * hist_rows + at % hist_rows

    offsets = []
    for step in range(PLANE):
        meta = queries[step][hist_rows:, LANES:].astype(jnp.float32)
        offset = meta[:, :hist_rows] * 16 + meta[:, hist_rows:]
        offsets.append(jnp.transpose(offset)[:, :1])
    offset = jnp.concatenate(offsets, axis=0).astype(jnp.int32)
    query_pos = positions((rows, 1), 0, 0)
    starts = query_pos - offset
    query = jnp.concatenate([queries[step][:hist_rows, :] for step in range(PLANE)], axis=0)
    totals = [jnp.zeros((rows, head_size), jnp.float32) for _ in range(heads)]
    for shift in range(shifts + 1):
        keys = blocks[shift][...]
        key_pos = positions((1, keys.shape[0]), 1, shift)
        inside = (key_pos <= query_pos) & (key_pos >= starts)
        for head in range(heads):
            window = slice(head * head_size, (head + 1) * head_size)
            logits = scale * lax.dot_general(
                query[:, window],
                keys[:, window],
                (((1,), (1,)), ((), ())),
                preferred_element_type=jnp.float32,
            )
            weights = jnp.where(inside, jax.nn.silu(logits) * (1.0 / WIN), 0.0)
            totals[head] += jnp.dot(
                weights.astype(jnp.bfloat16),
                keys[:, part + head * head_size : part + (head + 1) * head_size],
                preferred_element_type=jnp.float32,
            )
    for head in range(heads):
        window = slice(head * head_size, (head + 1) * head_size)
        out_ref[:, window] = totals[head].astype(jnp.bfloat16)


def mlp_kernel(row_hbm, up_hbm, down_hbm, out_hbm, *rest):
    parts, (row_ref, up_ref, down_ref, hidden_ref, sems) = rest[:PLANE], rest[PLANE:]
    windows = part_windows(parts[0].shape[1])
    hidden_size = up_ref.shape[1]
    half = hidden_size // 2
    quarter = hidden_size // 4
    loads = [(row_hbm, row_ref)]
    loads += [(up_hbm.at[:, w], up_ref.at[:, w]) for w in (slice(0, half), slice(half, None))]
    loads += [
        (down_hbm.at[pl.ds(at * quarter, quarter)], down_ref.at[pl.ds(at * quarter, quarter)])
        for at in range(4)
    ]
    saves = [(parts[step], out_hbm.at[:, windows[step]]) for step in range(PLANE)]
    copies = copies_of(loads + saves, sems)
    for copy in copies[:7]:
        copy.start()
    copies[0].wait()
    for at in range(0, hidden_size, TILE):
        if at % half == 0:
            copies[1 + at // half].wait()
        hidden = jnp.dot(
            row_ref[...], up_ref[:, at : at + TILE], preferred_element_type=jnp.float32
        )
        hidden_ref[:, at : at + TILE] = jax.nn.silu(hidden).astype(jnp.bfloat16)
    for copy in copies[3:7]:
        copy.wait()
    for step in range(PLANE):
        mixed = jnp.dot(
            hidden_ref[...], down_ref[:, windows[step]], preferred_element_type=jnp.float32
        )
        mixed = row_ref[:, windows[step]].astype(jnp.float32) + mixed
        parts[step][...] = mixed.astype(jnp.bfloat16)
        copies[7 + step].start()
    for copy in copies[7:]:
        copy.wait()


def place_kernel(hist_rows, store_rows, *refs):
    metas, out_ref = refs[:-1], refs[-1]
    plane, column = my_place()
    slots = metas[0].shape[0] // PLANE
    ids = []
    for meta_ref in metas:
        pieces = []
        for step in range(PLANE):
            meta = meta_ref[step * slots : (step + 1) * slots, :].astype(jnp.float32)
            pieces.append(meta[:, :hist_rows] * 256 + meta[:, hist_rows:])
        ids.append(jnp.concatenate(pieces, axis=1))
    pad = LANES - len(metas) * slots
    if pad:
        ids.append(jnp.zeros((pad, PLANE * hist_rows), jnp.float32))
    local = jnp.transpose(jnp.concatenate(ids, axis=0)).astype(jnp.int32)
    local = local - plane * (PLANE * store_rows)
    owned = (local >= 0) & (local < PLANE * store_rows)
    place = ((local // store_rows) ^ column) * store_rows + local % store_rows
    out_ref[...] = jnp.where(owned, place, -1)


def score_kernel(hist_rows, slots, at, first, *refs):
    user_ref, items, place_ref = refs[0], refs[1 : 1 + PLANE], refs[1 + PLANE]
    before_ref = None if first else refs[2 + PLANE]
    out_ref, dense_ref = refs[-2:]
    store_rows = items[0].shape[0]
    for step in range(PLANE):
        dense_ref[:, step * store_rows : (step + 1) * store_rows] = lax.dot_general(
            user_ref[...],
            items[step][...],
            (((1,), (1,)), ((), ())),
            preferred_element_type=jnp.float32,
        )
    for tile in range(PLANE):
        rows = slice(tile * hist_rows, (tile + 1) * hist_rows)
        place = place_ref[rows, :]
        lane_at = place & (LANES - 1)
        lane_of = lax.broadcasted_iota(jnp.int32, place.shape, 1) // slots
        mine = jnp.where((lane_of == at) & (place >= 0), place // LANES, -1)
        total = jnp.zeros(place.shape, jnp.float32) if first else before_ref[rows, :]
        for chunk in range(PLANE * store_rows // LANES):
            picked = jnp.take_along_axis(
                dense_ref[rows, chunk * LANES : (chunk + 1) * LANES],
                lane_at,
                axis=1,
                mode="promise_in_bounds",
            )
            total = jnp.where(mine == chunk, picked, total)
        out_ref[rows, :] = total


def send_kernel(hist_rows, slots, ordered, total_ref, out_ref):
    plane, column = my_place()
    turned = jnp.transpose(total_ref[...])
    half = slots // 2
    for at in range(out_ref.shape[0] // PLANE):
        for step in range(PLANE):
            lanes = slice(step * hist_rows, (step + 1) * hist_rows)
            block = jnp.concatenate(
                [
                    turned[at * slots : at * slots + half, lanes],
                    turned[at * slots + half : (at + 1) * slots, lanes],
                ],
                axis=1,
            )
            to_plane = plane ^ at if ordered else at
            out_ref[to_plane * PLANE + (column ^ step)] = block


def finish_kernel(part_ref, count_ref, out_ref):
    total = part_ref[0]
    for at in range(1, part_ref.shape[0]):
        total = total + part_ref[at]
    hist_rows = out_ref.shape[1]
    total = jnp.concatenate([total[:, :hist_rows], total[:, hist_rows:]], axis=0)
    live = lax.broadcasted_iota(jnp.int32, total.shape, 0) < count_ref[...]
    out_ref[...] = jnp.where(live, total, 0.0)


def per_device(
    item_rows, item_slot, w_up, w_down, events, w_query, history_kv, window_start, cand, cand_count
):
    block_count = lax.axis_size("blk")
    planes = block_count // PLANE
    plane, _ = my_place()
    hist_rows = events.shape[0]
    store_rows, width = item_rows.shape
    hidden_size = w_up.shape[1]
    cand_slots = cand.shape[1]
    att = history_kv.shape[2]
    part = att // PLANE
    rows = PLANE * hist_rows
    bf16 = jnp.bfloat16
    reach = WIN // hist_rows - 1
    shifts = -(-reach // PLANE)
    steps = range(1, PLANE)

    kv_own = call(
        kv_pieces_kernel,
        [jax.ShapeDtypeStruct((hist_rows, 2 * part), bf16)] * PLANE,
        [history_kv],
        [pltpu.VMEM((hist_rows, att), bf16)] * 2,
    )
    kv_plane = [kv_own[0]] + [in_plane(kv_own[step], step) for step in steps]
    query_own = call(
        query_kernel,
        [jax.ShapeDtypeStruct((hist_rows + cand_slots, part), bf16)] * PLANE,
        [events, w_query, cand.T, item_slot.reshape(-1, LANES), window_start.reshape(1, -1)],
        [
            pltpu.VMEM(events.shape, bf16),
            pltpu.VMEM(w_query.shape, bf16),
            pltpu.VMEM((cand_slots, hist_rows), jnp.int32),
            pltpu.VMEM((item_slot.shape[0] // LANES, LANES), jnp.int32),
            pltpu.VMEM((1, hist_rows), jnp.int32),
            pltpu.VMEM((hist_rows, att), bf16),
            pltpu.SemaphoreType.DMA((5,)),
        ],
        flops=2 * hist_rows * width * att,
        grant=QUERY_GRANT,
    )
    query_plane = [query_own[0]] + [in_plane(query_own[step], step) for step in steps]
    kv_all, kv_late = call(
        join_kernel,
        [
            jax.ShapeDtypeStruct((rows, 2 * part), bf16),
            jax.ShapeDtypeStruct((rows - hist_rows, 2 * part), bf16),
        ],
        kv_plane,
    )
    kv_blocks = [kv_all] + [
        forward(kv_late if shift * PLANE > reach else kv_all, shift)
        for shift in range(1, shifts + 1)
    ]

    meta = call(
        functools.partial(collect_kernel, hist_rows),
        jax.ShapeDtypeStruct((PLANE * cand_slots, LANES), bf16),
        query_plane,
    )
    metas = [meta] + [swap(meta, step) for step in range(1, planes)]

    mlp = call(
        mlp_kernel,
        [jax.ShapeDtypeStruct((store_rows, width), bf16)]
        + [jax.ShapeDtypeStruct((store_rows, part), bf16)] * PLANE,
        [item_rows, w_up, w_down],
        [
            pltpu.VMEM((store_rows, width), bf16),
            pltpu.VMEM((width, hidden_size), bf16),
            pltpu.VMEM((hidden_size, width), bf16),
            pltpu.VMEM((store_rows, hidden_size), bf16),
            pltpu.SemaphoreType.DMA((7 + PLANE,)),
        ],
        flops=4 * store_rows * width * hidden_size,
        grant=MLP_GRANT,
        first_out=HBM_SPEC,
    )
    item_out, item_parts = mlp[0], mlp[1:]
    item_plane = [item_parts[0]] + [in_plane(item_parts[step], step) for step in steps]

    user = call(
        functools.partial(attend_kernel, hist_rows, shifts),
        jax.ShapeDtypeStruct((rows, part), bf16),
        query_plane + kv_blocks,
        flops=4 * rows * rows * (shifts + 1) * part,
    )
    users = [user]
    for step in range(1, planes):
        bit = step & -step
        users.append(swap(users[step - bit], bit))
    together = min(planes, LANES // cand_slots, 4)
    results = []
    for first in range(0, planes, together):
        place = call(
            functools.partial(place_kernel, hist_rows, store_rows),
            jax.ShapeDtypeStruct((rows, LANES), jnp.int32),
            metas[first : first + together],
        )
        total = []
        for at in sorted(range(together), key=lambda at: (at == 3, at == 1)):
            total = [
                call(
                    functools.partial(score_kernel, hist_rows, cand_slots, at, not total),
                    jax.ShapeDtypeStruct((rows, LANES), jnp.float32),
                    [users[first + at]] + item_plane + [place] + total,
                    [pltpu.VMEM((rows, PLANE * store_rows), jnp.float32)],
                    flops=2 * rows * part * PLANE * store_rows,
                )
            ]
        results.append(
            call(
                functools.partial(send_kernel, hist_rows, cand_slots, planes == together),
                jax.ShapeDtypeStruct(
                    (together * PLANE, cand_slots // 2, 2 * hist_rows), jnp.float32
                ),
                total,
            )
        )
    if len(results) == 1:
        partial = results[0]
    else:
        order = plane ^ jnp.arange(planes, dtype=jnp.int32)
        partial = jnp.concatenate(results).reshape(planes, PLANE, cand_slots // 2, 2 * hist_rows)
        partial = partial[order].reshape(block_count, cand_slots // 2, 2 * hist_rows)
    gathered = lax.all_to_all(partial, "blk", split_axis=0, concat_axis=0, tiled=True)
    scores = call(
        finish_kernel,
        jax.ShapeDtypeStruct((cand_slots, hist_rows), jnp.float32),
        [gathered, cand_count.reshape(1, -1)],
    )
    return (item_out, scores.T)


def solution(mesh):
    in_specs = (
        P(("groups", "blk"), None),
        P("groups"),
        P(),
        P(),
        P(("groups", "blk"), None),
        P(),
        P(("groups", "blk"), None, None),
        P(("groups", "blk")),
        P(("groups", "blk"), None),
        P(("groups", "blk")),
    )
    out_specs = (P(("groups", "blk"), None), P(("groups", "blk"), None))
    return jax.shard_map(
        per_device, mesh=mesh, in_specs=in_specs, out_specs=out_specs, check_vma=False
    )
```

profile of v0, /device:TPU:0, one launch (start us, length us, event | category | flops | bytes accessed | tf_op | source)
XLA Modules:
  0.0 66.3 jit_solution(973351171926471058)
XLA Ops:
  0.6 0.0 copy-start.1
  0.6 0.9 %copy-done.1 = bf16[64,2,1024]{2,1,0:T(2,128)(2,1)S(1)} copy-done((bf16[64,2,1024]{2,1,0:T(2,128)(2,1)S(1)}, bf16[64,2,1024]{2,1,0:T(2,128)(2,1)}, u32[]{:S(2)}) %copy-start.1) | copy-done | bytes 262168
  1.6 0.6 shard_map.115
  2.2 0.6 collective-permute-start.3
  2.8 2.6 %collective-permute-start.4 = (bf16[64,512]{1,0:T(8,128)(2,1)S(1)}, bf16[64,512]{1,0:T(8,128)(2,1)S(1)}, u32[]{:S(2)}, u32[]{:S(2)}) collective-permute-start(bf16[64,512]{1,0:T(8,128)(2,1)S(1)} %get-tuple-element.24), channel_id=1, source_target_pairs={{0,2},{1,3},{2,0},{3,1},{4,6},{5,7},{6,4},{7,5},{8,10},{9,11},{10,... | collective-permute-start | bytes 196616 | tf_op jit(solution)/shard_map/ppermute | solution.py:43
  5.4 0.0 collective-permute-start.5
  5.4 2.9 %shard_map.114 = (bf16[80,256]{1,0:T(8,128)(2,1)}, bf16[80,256]{1,0:T(8,128)(2,1)}, bf16[80,256]{1,0:T(8,128)(2,1)}, bf16[80,256]{1,0:T(8,128)(2,1)}) custom-call(bf16[64,1024]{1,0:T(8,128)(2,1)} %event_hbm.1, bf16[1024,1024]{1,0:T(8,128)(2,1)} %weight_hbm.1, s32[16,64]{1,0:T(8,128)} %bitcast.7, s32[64,128]{1,0:T(8,128)} %bitcast.6, s32[1,64]{1,0:T(1,128)} %bitcast.9), custom_call_target="tpu_custom_call" | custom-call | flops 134217728 | bytes 2265344 | tf_op jit(solution)/shard_map/pallas_call | solution.py:29
  8.3 0.2 collective-permute-start
  8.5 1.9 %collective-permute-start.1 = (bf16[80,256]{1,0:T(8,128)(2,1)}, bf16[80,256]{1,0:T(8,128)(2,1)S(1)}, u32[]{:S(2)}, u32[]{:S(2)}) collective-permute-start(bf16[80,256]{1,0:T(8,128)(2,1)} %get-tuple-element.20), channel_id=1, source_target_pairs={{0,2},{1,3},{2,0},{3,1},{4,6},{5,7},{6,4},{7,5},{8,10},{9,11},{10,... | collective-permute-start | bytes 122888 | tf_op jit(solution)/shard_map/ppermute | solution.py:43
  10.5 0.0 collective-permute-done.3.refs_1_
  10.5 0.0 collective-permute-start.2
  10.5 0.0 collective-permute-done.4.refs_2_
  10.5 0.0 collective-permute-done.5.refs_3_
  10.6 1.6 %collective-permute-start.6 = (bf16[256,512]{1,0:T(8,128)(2,1)S(1)}, bf16[256,512]{1,0:T(8,128)(2,1)S(1)}, u32[]{:S(2)}, u32[]{:S(2)}) collective-permute-start(bf16[256,512]{1,0:T(8,128)(2,1)S(1)} %get-tuple-element.26.refs_4_), channel_id=1, source_target_pairs={{0,4},{1,5},{2,6},{3,7},{4,8},{5,9},{6,10},{7,11},{8,12},{9,13},{1... | collective-permute-start | bytes 786440 | tf_op jit(solution)/shard_map/ppermute | solution.py:48
  12.2 0.0 copy-start.2
  12.2 2.6 %collective-permute-start.7 = (bf16[192,512]{1,0:T(8,128)(2,1)S(1)}, bf16[192,512]{1,0:T(8,128)(2,1)S(1)}, u32[]{:S(2)}, u32[]{:S(2)}) collective-permute-start(bf16[192,512]{1,0:T(8,128)(2,1)S(1)} %get-tuple-element.27), channel_id=1, source_target_pairs={{0,8},{1,9},{2,10},{3,11},{4,12},{5,13},{6,14},{7,15},{8,0},{9,1},... | collective-permute-start | bytes 589832 | tf_op jit(solution)/shard_map/ppermute | solution.py:48
  14.8 8.7 %shard_map.113 = (bf16[512,1024]{1,0:T(8,128)(2,1)}, bf16[512,256]{1,0:T(8,128)(2,1)}, bf16[512,256]{1,0:T(8,128)(2,1)}, bf16[512,256]{1,0:T(8,128)(2,1)}, bf16[512,256]{1,0:T(8,128)(2,1)}) custom-call(bf16[512,1024]{1,0:T(8,128)(2,1)} %row_hbm.1, bf16[1024,2048]{1,0:T(8,128)(2,1)} %up_hbm.1, bf16[2048,1024]{1,0:T(8,128)(2,1)} %down_hbm.1), custom_call_target="tpu_custom_call" | custom-call | flops 4294967296 | bytes 9437184 | tf_op jit(solution)/shard_map/pallas_call | solution.py:29
  23.5 0.0 copy-start.3
  23.5 0.0 collective-permute-done.refs_1_
  23.5 0.1 collective-permute-start.10
  23.6 0.0 collective-permute-done.1.refs_2_
  23.6 1.5 %collective-permute-start.11 = (bf16[512,256]{1,0:T(8,128)(2,1)}, bf16[512,256]{1,0:T(8,128)(2,1)S(1)}, u32[]{:S(2)}, u32[]{:S(2)}) collective-permute-start(bf16[512,256]{1,0:T(8,128)(2,1)} %get-tuple-element.30), channel_id=1, source_target_pairs={{0,2},{1,3},{2,0},{3,1},{4,6},{5,7},{6,4},{7,5},{8,10},{9,11},{10,... | collective-permute-start | bytes 786440 | tf_op jit(solution)/shard_map/ppermute | solution.py:43
  25.2 0.0 collective-permute-done.2.refs_3_
  25.2 0.3 collective-permute-start.12
  25.4 4.3 %collective-permute-done.7.refs_6_ = bf16[192,512]{1,0:T(8,128)(2,1)S(1)} collective-permute-done((bf16[192,512]{1,0:T(8,128)(2,1)S(1)}, bf16[192,512]{1,0:T(8,128)(2,1)S(1)}, u32[]{:S(2)}, u32[]{:S(2)}) %collective-permute-start.7) | collective-permute-done | bytes 196640 | tf_op jit(solution)/shard_map/ppermute | solution.py:48
  29.7 0.0 collective-permute-done.6.refs_5_
  29.7 0.0 copy-done.2
  29.7 1.0 %shard_map.117.refs_0_ = bf16[256,256]{1,0:T(8,128)(2,1)S(1)} custom-call(bf16[80,256]{1,0:T(8,128)(2,1)S(1)} %copy-done.2, bf16[80,256]{1,0:T(8,128)(2,1)S(1)} %collective-permute-done.refs_1_, bf16[80,256]{1,0:T(8,128)(2,1)S(1)} %collective-permute-done.1.refs_2_, bf16[80,256]{1,0:T(8,128)(2,1)S(1)} %collective-permute-done.2.refs_3_, ...), custom_call_target="tpu_custom_call" | custom-call | flops 201326592 | bytes 884736 | tf_op jit(solution)/shard_map/pallas_call | solution.py:29
  30.8 0.1 collective-permute-start.8
  30.9 2.2 %collective-permute-start.13 = (bf16[64,128]{1,0:T(8,128)(2,1)S(1)}, bf16[64,128]{1,0:T(8,128)(2,1)S(1)}, u32[]{:S(2)}, u32[]{:S(2)}) collective-permute-start(bf16[64,128]{1,0:T(8,128)(2,1)S(1)} %shard_map.118.refs_0_), channel_id=1, source_target_pairs={{0,4},{1,5},{2,6},{3,7},{4,0},{5,1},{6,2},{7,3},{8,12},{9,13},{10,... | collective-permute-start | bytes 49160 | tf_op jit(solution)/shard_map/ppermute | solution.py:53
  33.0 1.7 %collective-permute-done.13.refs_1_ = bf16[64,128]{1,0:T(8,128)(2,1)S(1)} collective-permute-done((bf16[64,128]{1,0:T(8,128)(2,1)S(1)}, bf16[64,128]{1,0:T(8,128)(2,1)S(1)}, u32[]{:S(2)}, u32[]{:S(2)}) %collective-permute-start.13) | collective-permute-done | bytes 16416 | tf_op jit(solution)/shard_map/ppermute | solution.py:53
  34.8 2.7 %collective-permute-start.14 = (bf16[64,128]{1,0:T(8,128)(2,1)S(1)}, bf16[64,128]{1,0:T(8,128)(2,1)S(1)}, u32[]{:S(2)}, u32[]{:S(2)}) collective-permute-start(bf16[64,128]{1,0:T(8,128)(2,1)S(1)} %shard_map.118.refs_0_), channel_id=1, source_target_pairs={{0,8},{1,9},{2,10},{3,11},{4,12},{5,13},{6,14},{7,15},{8,0},{9,1},... | collective-permute-start | bytes 49160 | tf_op jit(solution)/shard_map/ppermute | solution.py:53
  37.5 1.9 %collective-permute-done.14.refs_2_ = bf16[64,128]{1,0:T(8,128)(2,1)S(1)} collective-permute-done((bf16[64,128]{1,0:T(8,128)(2,1)S(1)}, bf16[64,128]{1,0:T(8,128)(2,1)S(1)}, u32[]{:S(2)}, u32[]{:S(2)}) %collective-permute-start.14) | collective-permute-done | bytes 16416 | tf_op jit(solution)/shard_map/ppermute | solution.py:53
  39.4 2.3 %collective-permute-start.15 = (bf16[64,128]{1,0:T(8,128)(2,1)S(1)}, bf16[64,128]{1,0:T(8,128)(2,1)S(1)}, u32[]{:S(2)}, u32[]{:S(2)}) collective-permute-start(bf16[64,128]{1,0:T(8,128)(2,1)S(1)} %shard_map.118.refs_0_), channel_id=1, source_target_pairs={{0,12},{1,13},{2,14},{3,15},{4,8},{5,9},{6,10},{7,11},{8,4},{9,5},... | collective-permute-start | bytes 49160 | tf_op jit(solution)/shard_map/ppermute | solution.py:53
  41.7 3.2 %collective-permute-done.15.refs_3_ = bf16[64,128]{1,0:T(8,128)(2,1)S(1)} collective-permute-done((bf16[64,128]{1,0:T(8,128)(2,1)S(1)}, bf16[64,128]{1,0:T(8,128)(2,1)S(1)}, u32[]{:S(2)}, u32[]{:S(2)}) %collective-permute-start.15) | collective-permute-done | bytes 16416 | tf_op jit(solution)/shard_map/ppermute | solution.py:53
  45.0 0.4 collective-permute-start.16
  45.4 0.0 collective-permute-done.8.refs_0_
  45.4 1.6 %collective-permute-start.9 = (bf16[256,256]{1,0:T(8,128)(2,1)S(1)}, bf16[256,256]{1,0:T(8,128)(2,1)S(1)}, u32[]{:S(2)}, u32[]{:S(2)}) collective-permute-start(bf16[256,256]{1,0:T(8,128)(2,1)S(1)} %collective-permute-done.8.refs_0_), channel_id=1, source_target_pairs={{0,4},{1,5},{2,6},{3,7},{4,0},{5,1},{6,2},{7,3},{8,12},{9,13},{10,... | collective-permute-start | bytes 393224 | tf_op jit(solution)/shard_map/ppermute | solution.py:53
  47.0 0.3 shard_map.119.refs_5_
  47.3 0.0 collective-permute-done.10.refs_2_
  47.4 0.0 collective-permute-done.11.refs_3_
  47.4 0.0 collective-permute-done.12.refs_4_
  47.4 0.0 copy-start
  47.4 0.9 %copy-done = bf16[512,256]{1,0:T(8,128)(2,1)S(1)} copy-done((bf16[512,256]{1,0:T(8,128)(2,1)S(1)}, bf16[512,256]{1,0:T(8,128)(2,1)}, u32[]{:S(2)}) %copy-start) | copy-done | bytes 262168
  48.3 1.4 %shard_map.120.refs_6_ = f32[256,128]{1,0:T(8,128)S(1)} custom-call(bf16[256,256]{1,0:T(8,128)(2,1)S(1)} %shard_map.117.refs_0_, bf16[512,256]{1,0:T(8,128)(2,1)S(1)} %copy-done, bf16[512,256]{1,0:T(8,128)(2,1)S(1)} %collective-permute-done.10.refs_2_, bf16[512,256]{1,0:T(8,128)(2,1)S(1)} %collective-permute-done.11.refs_3_, ...), custom_call_target="tpu_custom_call" | custom-call | flops 268435456 | bytes 1310720 | tf_op jit(solution)/shard_map/pallas_call | solution.py:29
  49.8 1.5 %shard_map.121.refs_6_ = f32[256,128]{1,0:T(8,128)S(1)} custom-call(bf16[256,256]{1,0:T(8,128)(2,1)S(1)} %collective-permute-done.8.refs_0_, bf16[512,256]{1,0:T(8,128)(2,1)S(1)} %copy-done, bf16[512,256]{1,0:T(8,128)(2,1)S(1)} %collective-permute-done.10.refs_2_, bf16[512,256]{1,0:T(8,128)(2,1)S(1)} %collective-permute-done.11.refs_3_, ...), custom_call_target="tpu_custom_call" | custom-call | flops 268435456 | bytes 1441792 | tf_op jit(solution)/shard_map/pallas_call | solution.py:29
  51.2 0.0 collective-permute-done.16.refs_0_
  51.2 1.5 %shard_map.122.refs_6_ = f32[256,128]{1,0:T(8,128)S(1)} custom-call(bf16[256,256]{1,0:T(8,128)(2,1)S(1)} %collective-permute-done.16.refs_0_, bf16[512,256]{1,0:T(8,128)(2,1)S(1)} %copy-done, bf16[512,256]{1,0:T(8,128)(2,1)S(1)} %collective-permute-done.10.refs_2_, bf16[512,256]{1,0:T(8,128)(2,1)S(1)} %collective-permute-done.11.refs_3_, ...), custom_call_target="tpu_custom_call" | custom-call | flops 268435456 | bytes 1441792 | tf_op jit(solution)/shard_map/pallas_call | solution.py:29
  52.7 0.0 collective-permute-done.9.refs_0_
  52.7 1.4 %shard_map.123.total_ref = f32[256,128]{1,0:T(8,128)S(1)} custom-call(bf16[256,256]{1,0:T(8,128)(2,1)S(1)} %collective-permute-done.9.refs_0_, bf16[512,256]{1,0:T(8,128)(2,1)S(1)} %copy-done, bf16[512,256]{1,0:T(8,128)(2,1)S(1)} %collective-permute-done.10.refs_2_, bf16[512,256]{1,0:T(8,128)(2,1)S(1)} %collective-permute-done.11.refs_3_, ...), custom_call_target="tpu_custom_call" | custom-call | flops 268435456 | bytes 1441792 | tf_op jit(solution)/shard_map/pallas_call | solution.py:29
  54.2 0.2 shard_map.124
  54.3 11.3 %all_to_all.5.part_ref = f32[16,8,128]{2,1,0:T(8,128)S(1)} all-to-all(f32[16,8,128]{2,1,0:T(8,128)S(1)} %shard_map.124), channel_id=1, replica_groups=mesh['groups'=2,'blk'=16] {'blk'}, dimensions={0} | all-to-all | bytes 131072 | tf_op jit(solution)/shard_map/all_to_all | solution.py:444
  65.6 0.0 copy-done.3
  65.7 0.7 %shard_map.125 = f32[16,64]{1,0:T(8,128)} custom-call(f32[16,8,128]{2,1,0:T(8,128)S(1)} %all_to_all.5.part_ref, s32[1,64]{1,0:T(1,128)S(1)} %bitcast.5), custom_call_target="tpu_custom_call" | custom-call | bytes 65792 | tf_op jit(solution)/shard_map/pallas_call | solution.py:29
  (2 shorter events, 0.0 us)
Async XLA Ops:
  0.6 1.0 %copy-start.1 = (bf16[64,2,1024]{2,1,0:T(2,128)(2,1)S(1)}, bf16[64,2,1024]{2,1,0:T(2,128)(2,1)}, u32[]{:S(2)}) copy-start(bf16[64,2,1024]{2,1,0:T(2,128)(2,1)} %kv_ref.1) | copy-start | bytes 786436
  2.2 8.3 %collective-permute-start.3 = (bf16[64,512]{1,0:T(8,128)(2,1)S(1)}, bf16[64,512]{1,0:T(8,128)(2,1)S(1)}, u32[]{:S(2)}, u32[]{:S(2)}) collective-permute-start(bf16[64,512]{1,0:T(8,128)(2,1)S(1)} %get-tuple-element.23), channel_id=1, source_target_pairs={{0,1},{1,0},{2,3},{3,2},{4,5},{5,4},{6,7},{7,6},{8,9},{9,8},{10,11... | collective-permute-start | bytes 196616 | tf_op jit(solution)/shard_map/ppermute | solution.py:43
  2.8 7.7 %collective-permute-start.4 = (bf16[64,512]{1,0:T(8,128)(2,1)S(1)}, bf16[64,512]{1,0:T(8,128)(2,1)S(1)}, u32[]{:S(2)}, u32[]{:S(2)}) collective-permute-start(bf16[64,512]{1,0:T(8,128)(2,1)S(1)} %get-tuple-element.24), channel_id=1, source_target_pairs={{0,2},{1,3},{2,0},{3,1},{4,6},{5,7},{6,4},{7,5},{8,10},{9,11},{10,... | collective-permute-start | bytes 196616 | tf_op jit(solution)/shard_map/ppermute | solution.py:43
  5.4 5.1 %collective-permute-start.5 = (bf16[64,512]{1,0:T(8,128)(2,1)S(1)}, bf16[64,512]{1,0:T(8,128)(2,1)S(1)}, u32[]{:S(2)}, u32[]{:S(2)}) collective-permute-start(bf16[64,512]{1,0:T(8,128)(2,1)S(1)} %get-tuple-element.25), channel_id=1, source_target_pairs={{0,3},{1,2},{2,1},{3,0},{4,7},{5,6},{6,5},{7,4},{8,11},{9,10},{10,... | collective-permute-start | bytes 196616 | tf_op jit(solution)/shard_map/ppermute | solution.py:43
  8.3 15.2 %collective-permute-start = (bf16[80,256]{1,0:T(8,128)(2,1)}, bf16[80,256]{1,0:T(8,128)(2,1)S(1)}, u32[]{:S(2)}, u32[]{:S(2)}) collective-permute-start(bf16[80,256]{1,0:T(8,128)(2,1)} %get-tuple-element.19), channel_id=1, source_target_pairs={{0,1},{1,0},{2,3},{3,2},{4,5},{5,4},{6,7},{7,6},{8,9},{9,8},{10,11... | collective-permute-start | bytes 122888 | tf_op jit(solution)/shard_map/ppermute | solution.py:43
  8.5 15.1 %collective-permute-start.1 = (bf16[80,256]{1,0:T(8,128)(2,1)}, bf16[80,256]{1,0:T(8,128)(2,1)S(1)}, u32[]{:S(2)}, u32[]{:S(2)}) collective-permute-start(bf16[80,256]{1,0:T(8,128)(2,1)} %get-tuple-element.20), channel_id=1, source_target_pairs={{0,2},{1,3},{2,0},{3,1},{4,6},{5,7},{6,4},{7,5},{8,10},{9,11},{10,... | collective-permute-start | bytes 122888 | tf_op jit(solution)/shard_map/ppermute | solution.py:43
  10.5 14.7 %collective-permute-start.2 = (bf16[80,256]{1,0:T(8,128)(2,1)}, bf16[80,256]{1,0:T(8,128)(2,1)S(1)}, u32[]{:S(2)}, u32[]{:S(2)}) collective-permute-start(bf16[80,256]{1,0:T(8,128)(2,1)} %get-tuple-element.21), channel_id=1, source_target_pairs={{0,3},{1,2},{2,1},{3,0},{4,7},{5,6},{6,5},{7,4},{8,11},{9,10},{10,... | collective-permute-start | bytes 122888 | tf_op jit(solution)/shard_map/ppermute | solution.py:43
  10.6 19.2 %collective-permute-start.6 = (bf16[256,512]{1,0:T(8,128)(2,1)S(1)}, bf16[256,512]{1,0:T(8,128)(2,1)S(1)}, u32[]{:S(2)}, u32[]{:S(2)}) collective-permute-start(bf16[256,512]{1,0:T(8,128)(2,1)S(1)} %get-tuple-element.26.refs_4_), channel_id=1, source_target_pairs={{0,4},{1,5},{2,6},{3,7},{4,8},{5,9},{6,10},{7,11},{8,12},{9,13},{1... | collective-permute-start | bytes 786440 | tf_op jit(solution)/shard_map/ppermute | solution.py:48
  12.2 17.5 %copy-start.2 = (bf16[80,256]{1,0:T(8,128)(2,1)S(1)}, bf16[80,256]{1,0:T(8,128)(2,1)}, u32[]{:S(2)}) copy-start(bf16[80,256]{1,0:T(8,128)(2,1)} %get-tuple-element.18.refs_0_) | copy-start | bytes 122884
  12.2 17.5 %collective-permute-start.7 = (bf16[192,512]{1,0:T(8,128)(2,1)S(1)}, bf16[192,512]{1,0:T(8,128)(2,1)S(1)}, u32[]{:S(2)}, u32[]{:S(2)}) collective-permute-start(bf16[192,512]{1,0:T(8,128)(2,1)S(1)} %get-tuple-element.27), channel_id=1, source_target_pairs={{0,8},{1,9},{2,10},{3,11},{4,12},{5,13},{6,14},{7,15},{8,0},{9,1},... | collective-permute-start | bytes 589832 | tf_op jit(solution)/shard_map/ppermute | solution.py:48
  23.5 42.2 %copy-start.3 = (s32[64]{0:T(128)S(1)}, s32[64]{0:T(128)}, u32[]{:S(2)}) copy-start(s32[64]{0:T(128)} %param.19) | copy-start | bytes 772
  23.5 23.8 %collective-permute-start.10 = (bf16[512,256]{1,0:T(8,128)(2,1)}, bf16[512,256]{1,0:T(8,128)(2,1)S(1)}, u32[]{:S(2)}, u32[]{:S(2)}) collective-permute-start(bf16[512,256]{1,0:T(8,128)(2,1)} %get-tuple-element.29), channel_id=1, source_target_pairs={{0,1},{1,0},{2,3},{3,2},{4,5},{5,4},{6,7},{7,6},{8,9},{9,8},{10,11... | collective-permute-start | bytes 786440 | tf_op jit(solution)/shard_map/ppermute | solution.py:43
  23.6 23.7 %collective-permute-start.11 = (bf16[512,256]{1,0:T(8,128)(2,1)}, bf16[512,256]{1,0:T(8,128)(2,1)S(1)}, u32[]{:S(2)}, u32[]{:S(2)}) collective-permute-start(bf16[512,256]{1,0:T(8,128)(2,1)} %get-tuple-element.30), channel_id=1, source_target_pairs={{0,2},{1,3},{2,0},{3,1},{4,6},{5,7},{6,4},{7,5},{8,10},{9,11},{10,... | collective-permute-start | bytes 786440 | tf_op jit(solution)/shard_map/ppermute | solution.py:43
  25.2 22.2 %collective-permute-start.12 = (bf16[512,256]{1,0:T(8,128)(2,1)}, bf16[512,256]{1,0:T(8,128)(2,1)S(1)}, u32[]{:S(2)}, u32[]{:S(2)}) collective-permute-start(bf16[512,256]{1,0:T(8,128)(2,1)} %get-tuple-element.31), channel_id=1, source_target_pairs={{0,3},{1,2},{2,1},{3,0},{4,7},{5,6},{6,5},{7,4},{8,11},{9,10},{10,... | collective-permute-start | bytes 786440 | tf_op jit(solution)/shard_map/ppermute | solution.py:43
  30.8 14.6 %collective-permute-start.8 = (bf16[256,256]{1,0:T(8,128)(2,1)S(1)}, bf16[256,256]{1,0:T(8,128)(2,1)S(1)}, u32[]{:S(2)}, u32[]{:S(2)}) collective-permute-start(bf16[256,256]{1,0:T(8,128)(2,1)S(1)} %shard_map.117.refs_0_), channel_id=1, source_target_pairs={{0,8},{1,9},{2,10},{3,11},{4,12},{5,13},{6,14},{7,15},{8,0},{9,1},... | collective-permute-start | bytes 393224 | tf_op jit(solution)/shard_map/ppermute | solution.py:53
  30.9 3.9 %collective-permute-start.13 = (bf16[64,128]{1,0:T(8,128)(2,1)S(1)}, bf16[64,128]{1,0:T(8,128)(2,1)S(1)}, u32[]{:S(2)}, u32[]{:S(2)}) collective-permute-start(bf16[64,128]{1,0:T(8,128)(2,1)S(1)} %shard_map.118.refs_0_), channel_id=1, source_target_pairs={{0,4},{1,5},{2,6},{3,7},{4,0},{5,1},{6,2},{7,3},{8,12},{9,13},{10,... | collective-permute-start | bytes 49160 | tf_op jit(solution)/shard_map/ppermute | solution.py:53
  34.8 4.6 %collective-permute-start.14 = (bf16[64,128]{1,0:T(8,128)(2,1)S(1)}, bf16[64,128]{1,0:T(8,128)(2,1)S(1)}, u32[]{:S(2)}, u32[]{:S(2)}) collective-permute-start(bf16[64,128]{1,0:T(8,128)(2,1)S(1)} %shard_map.118.refs_0_), channel_id=1, source_target_pairs={{0,8},{1,9},{2,10},{3,11},{4,12},{5,13},{6,14},{7,15},{8,0},{9,1},... | collective-permute-start | bytes 49160 | tf_op jit(solution)/shard_map/ppermute | solution.py:53
  39.4 5.5 %collective-permute-start.15 = (bf16[64,128]{1,0:T(8,128)(2,1)S(1)}, bf16[64,128]{1,0:T(8,128)(2,1)S(1)}, u32[]{:S(2)}, u32[]{:S(2)}) collective-permute-start(bf16[64,128]{1,0:T(8,128)(2,1)S(1)} %shard_map.118.refs_0_), channel_id=1, source_target_pairs={{0,12},{1,13},{2,14},{3,15},{4,8},{5,9},{6,10},{7,11},{8,4},{9,5},... | collective-permute-start | bytes 49160 | tf_op jit(solution)/shard_map/ppermute | solution.py:53
  45.0 6.3 %collective-permute-start.16 = (bf16[256,256]{1,0:T(8,128)(2,1)S(1)}, bf16[256,256]{1,0:T(8,128)(2,1)S(1)}, u32[]{:S(2)}, u32[]{:S(2)}) collective-permute-start(bf16[256,256]{1,0:T(8,128)(2,1)S(1)} %shard_map.117.refs_0_), channel_id=1, source_target_pairs={{0,4},{1,5},{2,6},{3,7},{4,0},{5,1},{6,2},{7,3},{8,12},{9,13},{10,... | collective-permute-start | bytes 393224 | tf_op jit(solution)/shard_map/ppermute | solution.py:53
  45.4 7.3 %collective-permute-start.9 = (bf16[256,256]{1,0:T(8,128)(2,1)S(1)}, bf16[256,256]{1,0:T(8,128)(2,1)S(1)}, u32[]{:S(2)}, u32[]{:S(2)}) collective-permute-start(bf16[256,256]{1,0:T(8,128)(2,1)S(1)} %collective-permute-done.8.refs_0_), channel_id=1, source_target_pairs={{0,4},{1,5},{2,6},{3,7},{4,0},{5,1},{6,2},{7,3},{8,12},{9,13},{10,... | collective-permute-start | bytes 393224 | tf_op jit(solution)/shard_map/ppermute | solution.py:53
  47.4 1.0 %copy-start = (bf16[512,256]{1,0:T(8,128)(2,1)S(1)}, bf16[512,256]{1,0:T(8,128)(2,1)}, u32[]{:S(2)}) copy-start(bf16[512,256]{1,0:T(8,128)(2,1)} %get-tuple-element.28.refs_1_) | copy-start | bytes 786436
where the time goes:
time: 66.6 us; the launch traced here: 66.3 us
  starting transfers between devices  20.8 us (31%)
  Pallas kernels  20.3 us (30%)
  blocking collectives  11.3 us (17%)
  waiting for transfers between devices  11.2 us (17%)
  local copies, waits for them, and re-layouts  1.9 us (3%)
  between operations  0.8 us (1%)
    pallas_call x13, Pallas kernels, call(): pl.pallas_call(body, out_shape=out_shape, in_specs=[HBM_SPEC if grant els...  20.3 us
    all_to_all x1, blocking collectives, per_device(): lax.all_to_all(partial, 'blk', split_axis=0, concat_axis=0, tiled=True)  11.3 us
    ppermute x6, starting transfers between devices, swap(): lax.ppermute(value, 'blk', [(s, s ^ step * PLANE) for s in range(count)])  9.31 us
    ppermute x9, starting transfers between devices, in_plane(): return lax.ppermute(value, 'blk', pairs)  7.28 us
    ppermute x6, waiting for transfers between devices, swap(): lax.ppermute(value, 'blk', [(s, s ^ step * PLANE) for s in range(count)])  6.9 us
    ppermute x2, waiting for transfers between devices, forward(): lax.ppermute(value, 'blk', [(s, (s + step * PLANE) % count) for s in rang...  4.27 us
    ppermute x2, starting transfers between devices, forward(): lax.ppermute(value, 'blk', [(s, (s + step * PLANE) % count) for s in rang...  4.22 us
    unnamed x8, local copies, waits for them, and re-layouts  1.9 us
  transfers between devices with their start and end apart: 17, of which 4 were waited for; matrix products, arithmetic and copies ran while one was open for 0% of the time, Pallas kernels for 26%

commit v1 on v0

v1 whole, which is shorter than its diff:
```python
import functools

import jax
import jax.numpy as jnp
from jax import lax
from jax.experimental import pallas as pl
from jax.experimental.pallas import tpu as pltpu
from jax.sharding import PartitionSpec as P


HEADS = 8
WIN = 512
PLANE = 4
LANES = 128
TILE = 512

VMEM_SPEC = pl.BlockSpec(memory_space=pltpu.VMEM)
HBM_SPEC = pl.BlockSpec(memory_space=pltpu.MemorySpace.HBM)
VMEM_LIMIT = 24 * 1024 * 1024
COVER = 6_000_000_000


def call(body, out_shape, args, scratch=(), flops=0, first_out=None):
    size = sum(a.size * a.dtype.itemsize for a in args)
    out_specs = jax.tree.map(lambda _: VMEM_SPEC, out_shape)
    if first_out is not None:
        out_specs[0] = first_out
    return pl.pallas_call(
        body,
        out_shape=out_shape,
        in_specs=[VMEM_SPEC] * len(args),
        out_specs=out_specs,
        scratch_shapes=list(scratch),
        compiler_params=pltpu.CompilerParams(vmem_limit_bytes=VMEM_LIMIT),
        cost_estimate=pl.CostEstimate(flops=flops, bytes_accessed=size, transcendentals=0),
    )(*args)


def in_plane(value, step):
    count = lax.axis_size("blk")
    pairs = [(s, (s // PLANE) * PLANE + ((s % PLANE) ^ step)) for s in range(count)]
    return lax.ppermute(value, "blk", pairs)


def forward(value, step):
    count = lax.axis_size("blk")
    return lax.ppermute(value, "blk", [(s, (s + step * PLANE) % count) for s in range(count)])


def swap(value, step):
    count = lax.axis_size("blk")
    return lax.ppermute(value, "blk", [(s, s ^ (step * PLANE)) for s in range(count)])


def my_place():
    index = lax.axis_index("blk")
    return index // PLANE, index % PLANE


def part_windows(part):
    column = my_place()[1]
    return [pl.ds(pl.multiple_of((column ^ step) * part, part), part) for step in range(PLANE)]


def copies_of(pairs, sems):
    return [
        pltpu.make_async_copy(source, target, sems.at[at])
        for at, (source, target) in enumerate(pairs)
    ]


def kv_pieces_kernel(kv_ref, *rest):
    outs, (key_buf, value_buf) = rest[:PLANE], rest[PLANE:]
    part = outs[0].shape[1] // 2
    windows = part_windows(part)
    key_buf[...] = kv_ref[:, 0, :]
    value_buf[...] = kv_ref[:, 1, :]
    for step in range(PLANE):
        outs[step][:, :part] = key_buf[:, windows[step]]
        outs[step][:, part:] = value_buf[:, windows[step]]


def query_kernel(event_ref, weight_ref, cand_ref, table_ref, start_ref, *rest):
    query_outs, query_buf = rest[:PLANE], rest[PLANE]
    index = lax.axis_index("blk")
    hist_rows = event_ref.shape[0]
    windows = part_windows(query_outs[0].shape[1])
    ids = cand_ref[...]
    ids = jnp.concatenate([ids, ids], axis=1)
    table_row = ids // LANES
    table_lane = ids % LANES

    def look(row, found):
        values = jnp.broadcast_to(table_ref[pl.ds(row, 1), :], ids.shape)
        picked = jnp.take_along_axis(values, table_lane, axis=1, mode="promise_in_bounds")
        return jnp.where(table_row == row, picked, found)

    slot = lax.fori_loop(0, table_ref.shape[0], look, jnp.zeros_like(ids), unroll=8)
    first_half = lax.broadcasted_iota(jnp.int32, ids.shape, 1) < hist_rows
    slot_meta = jnp.where(first_half, slot // 256, slot % 256)
    starts = start_ref[...]
    starts = jnp.concatenate([starts, starts], axis=1)
    place = index * hist_rows + lax.broadcasted_iota(jnp.int32, starts.shape, 1) % hist_rows
    reach = index * hist_rows + hist_rows - WIN
    offset = place - jnp.maximum(starts, reach)
    offset = jnp.broadcast_to(offset, ids.shape)
    offset_meta = jnp.where(first_half, offset // 16, offset % 16)
    meta = jnp.concatenate([slot_meta, offset_meta], axis=1)
    meta = meta.astype(jnp.float32).astype(jnp.bfloat16)
    query = jnp.dot(event_ref[...], weight_ref[...], preferred_element_type=jnp.float32)
    query_buf[...] = query.astype(jnp.bfloat16)
    for step in range(PLANE):
        query_outs[step][:hist_rows, :] = query_buf[:, windows[step]]
        query_outs[step][hist_rows:, :] = meta


def join_kernel(*refs):
    pieces, (rest_ref, late_ref) = refs[:PLANE], refs[PLANE:]
    column = my_place()[1]
    rows = pieces[0].shape[0]
    for step in range(1, PLANE):
        rest_ref[(step - 1) * rows : step * rows, :] = pieces[step][...]
    for block in range(1, PLANE):
        for step in range(PLANE):

            @pl.when((column ^ block) == step)
            def _(block=block, step=step):
                late_ref[(block - 1) * rows : block * rows, :] = pieces[step][...]


def key_positions(hist_rows, count, shift):
    plane, column = my_place()
    at = lax.broadcasted_iota(jnp.int32, (1, count), 1)
    block = at // hist_rows
    block = (column ^ block) if count == PLANE * hist_rows else 1 + block
    return ((plane - shift) * PLANE + block) * hist_rows + at % hist_rows


def query_positions(hist_rows):
    plane, column = my_place()
    at = lax.broadcasted_iota(jnp.int32, (PLANE * hist_rows, 1), 0)
    return (plane * PLANE + (column ^ (at // hist_rows))) * hist_rows + at % hist_rows


def add_attention(total_ref, query, query_pos, offset, keys, key_pos):
    part = query.shape[1]
    head_size = part * PLANE // HEADS
    inside = (key_pos <= query_pos) & (key_pos >= query_pos - offset)
    for head in range(part // head_size):
        window = slice(head * head_size, (head + 1) * head_size)
        logits = head_size**-0.5 * lax.dot_general(
            query[:, window],
            keys[:, window],
            (((1,), (1,)), ((), ())),
            preferred_element_type=jnp.float32,
        )
        weights = jnp.where(inside, jax.nn.silu(logits) * (1.0 / WIN), 0.0)
        total_ref[:, window] += jnp.dot(
            weights.astype(jnp.bfloat16),
            keys[:, part + head * head_size : part + (head + 1) * head_size],
            preferred_element_type=jnp.float32,
        )


def near_kernel(hist_rows, *refs):
    queries, blocks = refs[:PLANE], refs[PLANE:-4]
    total_ref, query_ref, offset_ref, meta_ref = refs[-4:]
    slots = queries[0].shape[0] - hist_rows
    part = queries[0].shape[1]
    for step in range(PLANE):
        rows = slice(step * hist_rows, (step + 1) * hist_rows)
        query_ref[rows, :] = queries[step][:hist_rows, :]
        meta = queries[step][hist_rows:, LANES:].astype(jnp.float32)
        offset = meta[:, :hist_rows] * 16 + meta[:, hist_rows:]
        offset = jnp.transpose(offset)[:, :1].astype(jnp.int32)
        offset_ref[rows, :] = jnp.broadcast_to(offset, (hist_rows, LANES))
        row, lane = divmod(step * LANES, part)
        meta_ref[row * slots : (row + 1) * slots, lane : lane + LANES] = queries[step][
            hist_rows:, :LANES
        ]
    total_ref[...] = jnp.zeros_like(total_ref)
    query_pos = query_positions(hist_rows)
    blocks = [block[...] for block in blocks]
    planes = [jnp.concatenate(blocks[:PLANE], axis=0)]
    planes += [jnp.concatenate(blocks[at : at + 2], axis=0) for at in range(PLANE, len(blocks), 2)]
    for shift, keys in enumerate(planes):
        key_pos = key_positions(hist_rows, keys.shape[0], shift)
        add_attention(total_ref, query_ref[...], query_pos, offset_ref[:, :1], keys, key_pos)


def far_kernel(
    hist_rows, shift, key_ref, before_ref, query_ref, offset_ref, meta_ref, out_ref, total_ref
):
    rows = total_ref.shape[0]
    total_ref[...] = before_ref[...]
    key_pos = key_positions(hist_rows, key_ref.shape[0], shift)
    add_attention(
        total_ref,
        query_ref[...],
        query_positions(hist_rows),
        offset_ref[:, :1],
        key_ref[...],
        key_pos,
    )
    out_ref[:rows, :] = total_ref[...].astype(jnp.bfloat16)
    out_ref[rows:, :] = meta_ref[...]


def mlp_kernel(row_ref, up_ref, down_ref, out_hbm, *rest):
    parts, (hidden_ref, sems) = rest[:PLANE], rest[PLANE:]
    windows = part_windows(parts[0].shape[1])
    saves = copies_of(
        [(parts[step], out_hbm.at[:, windows[step]]) for step in range(PLANE)], sems
    )
    for at in range(0, up_ref.shape[1], TILE):
        hidden = jnp.dot(
            row_ref[...], up_ref[:, at : at + TILE], preferred_element_type=jnp.float32
        )
        hidden_ref[:, at : at + TILE] = jax.nn.silu(hidden).astype(jnp.bfloat16)
    for step in range(PLANE):
        mixed = jnp.dot(
            hidden_ref[...], down_ref[:, windows[step]], preferred_element_type=jnp.float32
        )
        mixed = row_ref[:, windows[step]].astype(jnp.float32) + mixed
        parts[step][...] = mixed.astype(jnp.bfloat16)
        saves[step].start()
    for copy in saves:
        copy.wait()


def item_places(hist_rows, slots, store_rows, at, user_ref):
    plane, column = my_place()
    rows, part = PLANE * hist_rows, user_ref.shape[1]
    pieces = []
    for step in range(PLANE):
        row, lane = divmod(step * LANES, part)
        row = rows + row * slots
        meta = user_ref[row : row + slots, lane : lane + LANES].astype(jnp.float32)
        pieces.append(meta[:, :hist_rows] * 256 + meta[:, hist_rows:])
    ids = [jnp.concatenate(pieces, axis=1)]
    low, high = at * slots, LANES - (at + 1) * slots
    if low:
        ids.insert(0, jnp.zeros((low, rows), jnp.float32))
    if high:
        ids.append(jnp.zeros((high, rows), jnp.float32))
    local = jnp.transpose(jnp.concatenate(ids, axis=0)).astype(jnp.int32)
    local = local - plane * (PLANE * store_rows)
    owned = (local >= 0) & (local < PLANE * store_rows)
    owned &= lax.broadcasted_iota(jnp.int32, local.shape, 1) // slots == at
    place = ((local // store_rows) ^ column) * store_rows + local % store_rows
    return jnp.where(owned, place, -1)


def score_kernel(hist_rows, slots, at, first, *refs):
    user_ref, items = refs[0], refs[1 : 1 + PLANE]
    before_ref = None if first else refs[1 + PLANE]
    out_ref, dense_ref = refs[-2:]
    store_rows = items[0].shape[0]
    for step in range(PLANE):
        dense_ref[:, step * store_rows : (step + 1) * store_rows] = lax.dot_general(
            user_ref[: PLANE * hist_rows, :],
            items[step][...],
            (((1,), (1,)), ((), ())),
            preferred_element_type=jnp.float32,
        )
    places = item_places(hist_rows, slots, store_rows, at, user_ref)
    for tile in range(PLANE):
        rows = slice(tile * hist_rows, (tile + 1) * hist_rows)
        place = places[rows, :]
        lane_at = place & (LANES - 1)
        mine = place >> 7
        total = jnp.zeros(place.shape, jnp.float32) if first else before_ref[rows, :]
        for chunk in range(PLANE * store_rows // LANES):
            picked = jnp.take_along_axis(
                dense_ref[rows, chunk * LANES : (chunk + 1) * LANES],
                lane_at,
                axis=1,
                mode="promise_in_bounds",
            )
            total = jnp.where(mine == chunk, picked, total)
        out_ref[rows, :] = total


def send_kernel(hist_rows, slots, ordered, total_ref, out_ref):
    plane, column = my_place()
    turned = jnp.transpose(total_ref[...])
    half = slots // 2
    for at in range(out_ref.shape[0] // PLANE):
        for step in range(PLANE):
            lanes = slice(step * hist_rows, (step + 1) * hist_rows)
            block = jnp.concatenate(
                [
                    turned[at * slots : at * slots + half, lanes],
                    turned[at * slots + half : (at + 1) * slots, lanes],
                ],
                axis=1,
            )
            to_plane = plane ^ at if ordered else at
            out_ref[to_plane * PLANE + (column ^ step)] = block


def finish_kernel(part_ref, count_ref, out_ref):
    total = part_ref[0]
    for at in range(1, part_ref.shape[0]):
        total = total + part_ref[at]
    hist_rows = out_ref.shape[1]
    total = jnp.concatenate([total[:, :hist_rows], total[:, hist_rows:]], axis=0)
    live = lax.broadcasted_iota(jnp.int32, total.shape, 0) < count_ref[...]
    out_ref[...] = jnp.where(live, total, 0.0)


def per_device(
    item_rows, item_slot, w_up, w_down, events, w_query, history_kv, window_start, cand, cand_count
):
    block_count = lax.axis_size("blk")
    planes = block_count // PLANE
    plane, _ = my_place()
    hist_rows = events.shape[0]
    store_rows, width = item_rows.shape
    hidden_size = w_up.shape[1]
    cand_slots = cand.shape[1]
    att = history_kv.shape[2]
    part = att // PLANE
    rows = PLANE * hist_rows
    bf16 = jnp.bfloat16
    reach = WIN // hist_rows - 1
    shifts = -(-reach // PLANE)
    steps = range(1, PLANE)

    kv_own = call(
        kv_pieces_kernel,
        [jax.ShapeDtypeStruct((hist_rows, 2 * part), bf16)] * PLANE,
        [history_kv],
        [pltpu.VMEM((hist_rows, att), bf16)] * 2,
        flops=COVER,
    )
    kv_plane = [kv_own[0]] + [in_plane(kv_own[step], step) for step in steps]
    query_own = call(
        query_kernel,
        [jax.ShapeDtypeStruct((hist_rows + cand_slots, part), bf16)] * PLANE,
        [events, w_query, cand.T, item_slot.reshape(-1, LANES), window_start.reshape(1, -1)],
        [pltpu.VMEM((hist_rows, att), bf16)],
        flops=COVER,
    )
    query_plane = [query_own[0]] + [in_plane(query_own[step], step) for step in steps]
    kv_rest, kv_late = call(
        join_kernel, [jax.ShapeDtypeStruct((rows - hist_rows, 2 * part), bf16)] * 2, kv_plane
    )
    kv_near = list(kv_plane)
    for shift in range(1, shifts):
        kv_near += [forward(kv_plane[0], shift), forward(kv_rest, shift)]
    kv_far = forward(kv_late, shifts)

    mlp = call(
        mlp_kernel,
        [jax.ShapeDtypeStruct((store_rows, width), bf16)]
        + [jax.ShapeDtypeStruct((store_rows, part), bf16)] * PLANE,
        [item_rows, w_up, w_down],
        [
            pltpu.VMEM((store_rows, hidden_size), bf16),
            pltpu.SemaphoreType.DMA((PLANE,)),
        ],
        flops=4 * store_rows * width * hidden_size,
        first_out=HBM_SPEC,
    )
    item_out, item_parts = mlp[0], mlp[1:]
    item_plane = [item_parts[0]] + [in_plane(item_parts[step], step) for step in steps]

    near = call(
        functools.partial(near_kernel, hist_rows),
        [
            jax.ShapeDtypeStruct((rows, part), jnp.float32),
            jax.ShapeDtypeStruct((rows, part), bf16),
            jax.ShapeDtypeStruct((rows, LANES), jnp.int32),
            jax.ShapeDtypeStruct((PLANE * cand_slots * LANES // part, part), bf16),
        ],
        query_plane + kv_near,
        flops=4 * rows * rows * shifts * part,
    )
    user = call(
        functools.partial(far_kernel, hist_rows, shifts),
        jax.ShapeDtypeStruct((rows + near[3].shape[0], part), bf16),
        [kv_far, *near],
        [pltpu.VMEM((rows, part), jnp.float32)],
        flops=4 * rows * rows * part,
    )
    users = [user]
    for step in range(1, planes):
        bit = step & -step
        users.append(swap(users[step - bit], bit))
    together = min(planes, LANES // cand_slots, 4)
    results = []
    for first in range(0, planes, together):
        total = []
        for at in sorted(range(together), key=lambda at: (at == 3, at == 1)):
            total = [
                call(
                    functools.partial(score_kernel, hist_rows, cand_slots, at, not total),
                    jax.ShapeDtypeStruct((rows, LANES), jnp.float32),
                    [users[first + at]] + item_plane + total,
                    [pltpu.VMEM((rows, PLANE * store_rows), jnp.float32)],
                    flops=2 * rows * part * PLANE * store_rows,
                )
            ]
        results.append(
            call(
                functools.partial(send_kernel, hist_rows, cand_slots, planes == together),
                jax.ShapeDtypeStruct(
                    (together * PLANE, cand_slots // 2, 2 * hist_rows), jnp.float32
                ),
                total,
            )
        )
    if len(results) == 1:
        partial = results[0]
    else:
        order = plane ^ jnp.arange(planes, dtype=jnp.int32)
        partial = jnp.concatenate(results).reshape(planes, PLANE, cand_slots // 2, 2 * hist_rows)
        partial = partial[order].reshape(block_count, cand_slots // 2, 2 * hist_rows)
    gathered = lax.all_to_all(partial, "blk", split_axis=0, concat_axis=0, tiled=True)
    scores = call(
        finish_kernel,
        jax.ShapeDtypeStruct((cand_slots, hist_rows), jnp.float32),
        [gathered, cand_count.reshape(1, -1)],
    )
    return (item_out, scores.T)


def solution(mesh):
    in_specs = (
        P(("groups", "blk"), None),
        P("groups"),
        P(),
        P(),
        P(("groups", "blk"), None),
        P(),
        P(("groups", "blk"), None, None),
        P(("groups", "blk")),
        P(("groups", "blk"), None),
        P(("groups", "blk")),
    )
    out_specs = (P(("groups", "blk"), None), P(("groups", "blk"), None))
    return jax.shard_map(
        per_device, mesh=mesh, in_specs=in_specs, out_specs=out_specs, check_vma=False
    )
```

time: 66.6 us -> 57.7 us (0.87)
  starting transfers between devices: 20.8 us -> 14.3 us
  Pallas kernels: 20.3 us -> 16.1 us
  waiting for transfers between devices: 11.2 us -> 13.7 us
  local copies, waits for them, and re-layouts: 1.9 us -> 1.14 us
    ppermute x6 -> x3, starting transfers between devices: 9.31 us -> 2.31 us  [swap(): lax.ppermute(value, 'blk', [(s, s ^ step * PLANE) for s in range(count)])]
    pallas_call x13 -> x12, Pallas kernels: 20.3 us -> 16.1 us  [call(): pl.pallas_call(body, out_shape=out_shape, in_specs=[VMEM_SPEC] * len(args...]
    ppermute x2 -> x3, waiting for transfers between devices: 4.27 us -> 6.3 us  [forward(): lax.ppermute(value, 'blk', [(s, (s + step * PLANE) % count) for s in rang...]
    ppermute x2 -> x3, starting transfers between devices: 4.22 us -> 5.11 us  [forward(): lax.ppermute(value, 'blk', [(s, (s + step * PLANE) % count) for s in rang...]
    unnamed x8 -> x20, local copies, waits for them, and re-layouts: 1.9 us -> 1.14 us
    ppermute x6 -> x3, waiting for transfers between devices: 6.9 us -> 7.36 us  [swap(): lax.ppermute(value, 'blk', [(s, s ^ step * PLANE) for s in range(count)])]
  transfers between devices with their start and end apart: 17 -> 15, of which waited for: 4 -> 3; matrix products, arithmetic and copies ran while one was open for 0% -> 0% of each run, Pallas kernels for 26% -> 23%
where the time goes in v1:
time: 57.7 us; the launch traced here: 57.5 us
  Pallas kernels  16.1 us (28%)
  starting transfers between devices  14.3 us (25%)
  waiting for transfers between devices  13.7 us (24%)
  blocking collectives  11.5 us (20%)
  local copies, waits for them, and re-layouts  1.14 us (2%)
  between operations  0.81 us (1%)
    pallas_call x12, Pallas kernels, call(): pl.pallas_call(body, out_shape=out_shape, in_specs=[VMEM_SPEC] * len(args...  16.1 us
    all_to_all x1, blocking collectives, per_device(): lax.all_to_all(partial, 'blk', split_axis=0, concat_axis=0, tiled=True)  11.5 us
    ppermute x3, waiting for transfers between devices, swap(): lax.ppermute(value, 'blk', [(s, s ^ step * PLANE) for s in range(count)])  7.36 us
    ppermute x9, starting transfers between devices, in_plane(): return lax.ppermute(value, 'blk', pairs)  6.89 us
    ppermute x3, waiting for transfers between devices, forward(): lax.ppermute(value, 'blk', [(s, (s + step * PLANE) % count) for s in rang...  6.3 us
    ppermute x3, starting transfers between devices, forward(): lax.ppermute(value, 'blk', [(s, (s + step * PLANE) % count) for s in rang...  5.11 us
    ppermute x3, starting transfers between devices, swap(): lax.ppermute(value, 'blk', [(s, s ^ step * PLANE) for s in range(count)])  2.31 us
  transfers between devices with their start and end apart: 15, of which 3 were waited for; matrix products, arithmetic and copies ran while one was open for 0% of the time, Pallas kernels for 23%

profile of v1, /device:TPU:0, one launch (start us, length us, event | category | flops | bytes accessed | tf_op | source)
XLA Modules:
  0.0 57.5 jit_solution(3531293575622149950)
XLA Ops:
  0.6 0.0 copy-start.3
  0.6 0.0 copy-start.5
  0.7 1.1 %copy-done.5 = bf16[64,2,1024]{2,1,0:T(2,128)(2,1)S(1)} copy-done((bf16[64,2,1024]{2,1,0:T(2,128)(2,1)S(1)}, bf16[64,2,1024]{2,1,0:T(2,128)(2,1)}, u32[]{:S(2)}) %copy-start.5) | copy-done | bytes 262168
  1.7 0.0 copy-start.6
  1.7 0.0 copy-start.7
  1.7 0.0 copy-start.8
  1.7 0.0 copy-start.9
  1.8 0.6 %shard_map.114 = (bf16[64,512]{1,0:T(8,128)(2,1)S(1)}, bf16[64,512]{1,0:T(8,128)(2,1)S(1)}, bf16[64,512]{1,0:T(8,128)(2,1)S(1)}, bf16[64,512]{1,0:T(8,128)(2,1)S(1)}) custom-call(bf16[64,2,1024]{2,1,0:T(2,128)(2,1)S(1)} %copy-done.5), custom_call_target="tpu_custom_call" | custom-call | flops 6000000000 | bytes 262144 | tf_op jit(solution)/shard_map/pallas_call | solution.py:28
  2.4 0.6 collective-permute-start
  3.0 2.6 %collective-permute-start.1 = (bf16[64,512]{1,0:T(8,128)(2,1)S(1)}, bf16[64,512]{1,0:T(8,128)(2,1)S(1)}, u32[]{:S(2)}, u32[]{:S(2)}) collective-permute-start(bf16[64,512]{1,0:T(8,128)(2,1)S(1)} %get-tuple-element.24), channel_id=1, source_target_pairs={{0,2},{1,3},{2,0},{3,1},{4,6},{5,7},{6,4},{7,5},{8,10},{9,11},{10,... | collective-permute-start | bytes 196616 | tf_op jit(solution)/shard_map/ppermute | solution.py:42
  5.5 0.0 collective-permute-start.2
  5.6 0.0 copy-done.3
  5.6 0.0 copy-done.6
  5.6 0.0 copy-done.7
  5.6 0.0 copy-done.8
  5.6 0.0 copy-done.9
  5.6 0.0 copy-start.1
  5.6 0.0 copy-start.2
  5.6 0.0 copy-start.4
  5.6 1.3 %shard_map.116 = (bf16[80,256]{1,0:T(8,128)(2,1)S(1)}, bf16[80,256]{1,0:T(8,128)(2,1)S(1)}, bf16[80,256]{1,0:T(8,128)(2,1)S(1)}, bf16[80,256]{1,0:T(8,128)(2,1)S(1)}) custom-call(bf16[64,1024]{1,0:T(8,128)(2,1)S(1)} %copy-done.6, bf16[1024,1024]{1,0:T(8,128)(2,1)S(1)} %copy-done.3, s32[16,64]{1,0:T(8,128)S(1)} %bitcast.7, s32[64,128]{1,0:T(8,128)S(1)} %bitcast.6, ...), custom_call_target="tpu_custom_call" | custom-call | flops 6000000000 | bytes 2265344 | tf_op jit(solution)/shard_map/pallas_call | solution.py:28
  6.9 0.2 collective-permute-start.4
  7.2 2.0 %collective-permute-start.7 = (bf16[64,512]{1,0:T(8,128)(2,1)S(1)}, bf16[64,512]{1,0:T(8,128)(2,1)S(1)}, u32[]{:S(2)}, u32[]{:S(2)}) collective-permute-start(bf16[64,512]{1,0:T(8,128)(2,1)S(1)} %get-tuple-element.22.refs_0_.refs_4_), channel_id=1, source_target_pairs={{0,4},{1,5},{2,6},{3,7},{4,8},{5,9},{6,10},{7,11},{8,12},{9,13},{1... | collective-permute-start | bytes 196616 | tf_op jit(solution)/shard_map/ppermute | solution.py:47
  9.2 0.0 collective-permute-done.refs_1_.refs_5_
  9.2 1.5 %collective-permute-start.5 = (bf16[80,256]{1,0:T(8,128)(2,1)S(1)}, bf16[80,256]{1,0:T(8,128)(2,1)S(1)}, u32[]{:S(2)}, u32[]{:S(2)}) collective-permute-start(bf16[80,256]{1,0:T(8,128)(2,1)S(1)} %get-tuple-element.29), channel_id=1, source_target_pairs={{0,2},{1,3},{2,0},{3,1},{4,6},{5,7},{6,4},{7,5},{8,10},{9,11},{10,... | collective-permute-start | bytes 122888 | tf_op jit(solution)/shard_map/ppermute | solution.py:42
  10.7 0.0 collective-permute-done.1.refs_2_.refs_6_
  10.7 0.0 collective-permute-start.6
  10.7 0.0 collective-permute-done.2.refs_3_.refs_7_
  10.7 0.1 shard_map.115
  10.8 1.6 %collective-permute-start.8 = (bf16[192,512]{1,0:T(8,128)(2,1)S(1)}, bf16[192,512]{1,0:T(8,128)(2,1)S(1)}, u32[]{:S(2)}, u32[]{:S(2)}) collective-permute-start(bf16[192,512]{1,0:T(8,128)(2,1)S(1)} %get-tuple-element.31), channel_id=1, source_target_pairs={{0,4},{1,5},{2,6},{3,7},{4,8},{5,9},{6,10},{7,11},{8,12},{9,13},{1... | collective-permute-start | bytes 589832 | tf_op jit(solution)/shard_map/ppermute | solution.py:47
  12.4 0.0 collective-permute-done.4.refs_1_
  12.4 1.5 %collective-permute-start.3 = (bf16[192,512]{1,0:T(8,128)(2,1)S(1)}, bf16[192,512]{1,0:T(8,128)(2,1)S(1)}, u32[]{:S(2)}, u32[]{:S(2)}) collective-permute-start(bf16[192,512]{1,0:T(8,128)(2,1)S(1)} %get-tuple-element.26), channel_id=1, source_target_pairs={{0,8},{1,9},{2,10},{3,11},{4,12},{5,13},{6,14},{7,15},{8,0},{9,1},... | collective-permute-start | bytes 589832 | tf_op jit(solution)/shard_map/ppermute | solution.py:47
  13.9 0.0 copy-done.1
  13.9 0.0 copy-done.2
  13.9 0.0 copy-done.4
  13.9 5.4 %shard_map.113 = (bf16[512,1024]{1,0:T(8,128)(2,1)}, bf16[512,256]{1,0:T(8,128)(2,1)S(1)}, bf16[512,256]{1,0:T(8,128)(2,1)S(1)}, bf16[512,256]{1,0:T(8,128)(2,1)S(1)}, bf16[512,256]{1,0:T(8,128)(2,1)S(1)}) custom-call(bf16[512,1024]{1,0:T(8,128)(2,1)S(1)} %copy-done.4, bf16[1024,2048]{1,0:T(8,128)(2,1)S(1)} %copy-done.1, bf16[2048,1024]{1,0:T(8,128)(2,1)S(1)} %copy-done.2), custom_call_target="tpu_custom_call" | custom-call | flops 4294967296 | bytes 9437184 | tf_op jit(solution)/shard_map/pallas_call | solution.py:28
  19.3 0.0 copy-start
  19.3 0.0 collective-permute-done.5.refs_2_
  19.3 0.5 collective-permute-start.11
  19.9 0.0 collective-permute-done.6.refs_3_
  19.9 1.0 %collective-permute-start.12 = (bf16[512,256]{1,0:T(8,128)(2,1)S(1)}, bf16[512,256]{1,0:T(8,128)(2,1)S(1)}, u32[]{:S(2)}, u32[]{:S(2)}) collective-permute-start(bf16[512,256]{1,0:T(8,128)(2,1)S(1)} %get-tuple-element.38), channel_id=1, source_target_pairs={{0,2},{1,3},{2,0},{3,1},{4,6},{5,7},{6,4},{7,5},{8,10},{9,11},{10,... | collective-permute-start | bytes 786440 | tf_op jit(solution)/shard_map/ppermute | solution.py:42
  20.9 0.0 collective-permute-done.7.refs_8_
  20.9 0.4 collective-permute-start.13
  21.3 0.0 collective-permute-done.8.refs_9_
  21.3 0.9 %shard_map.117 = (f32[256,256]{1,0:T(8,128)S(1)}, bf16[256,256]{1,0:T(8,128)(2,1)S(1)}, s32[256,128]{1,0:T(8,128)S(1)}, bf16[32,256]{1,0:T(8,128)(2,1)S(1)}) custom-call(bf16[80,256]{1,0:T(8,128)(2,1)S(1)} %get-tuple-element.27.refs_0_, bf16[80,256]{1,0:T(8,128)(2,1)S(1)} %collective-permute-done.4.refs_1_, ...), custom_call_target="tpu_custom_call" | custom-call | flops 134217728 | bytes 688128 | tf_op jit(solution)/shard_map/pallas_call | solution.py:28
  22.2 6.3 %collective-permute-done.3.key_ref = bf16[192,512]{1,0:T(8,128)(2,1)S(1)} collective-permute-done((bf16[192,512]{1,0:T(8,128)(2,1)S(1)}, bf16[192,512]{1,0:T(8,128)(2,1)S(1)}, u32[]{:S(2)}, u32[]{:S(2)}) %collective-permute-start.3) | collective-permute-done | bytes 196640 | tf_op jit(solution)/shard_map/ppermute | solution.py:47
  28.5 0.6 shard_map.118.refs_0_
  29.0 0.1 collective-permute-start.9
  29.1 2.2 %collective-permute-start.14 = (bf16[288,256]{1,0:T(8,128)(2,1)S(1)}, bf16[288,256]{1,0:T(8,128)(2,1)S(1)}, u32[]{:S(2)}, u32[]{:S(2)}) collective-permute-start(bf16[288,256]{1,0:T(8,128)(2,1)S(1)} %shard_map.118.refs_0_), channel_id=1, source_target_pairs={{0,4},{1,5},{2,6},{3,7},{4,0},{5,1},{6,2},{7,3},{8,12},{9,13},{10,... | collective-permute-start | bytes 442376 | tf_op jit(solution)/shard_map/ppermute | solution.py:52
  31.4 6.5 %collective-permute-done.9.refs_0_ = bf16[288,256]{1,0:T(8,128)(2,1)S(1)} collective-permute-done((bf16[288,256]{1,0:T(8,128)(2,1)S(1)}, bf16[288,256]{1,0:T(8,128)(2,1)S(1)}, u32[]{:S(2)}, u32[]{:S(2)}) %collective-permute-start.9) | collective-permute-done | bytes 147488 | tf_op jit(solution)/shard_map/ppermute | solution.py:52
  37.8 0.0 collective-permute-start.10
  37.8 0.0 collective-permute-done.11.refs_2_
  37.8 0.0 collective-permute-done.12.refs_3_
  37.8 0.0 collective-permute-done.13.refs_4_
  37.9 1.6 %shard_map.119.refs_5_ = f32[256,128]{1,0:T(8,128)S(1)} custom-call(bf16[288,256]{1,0:T(8,128)(2,1)S(1)} %shard_map.118.refs_0_, bf16[512,256]{1,0:T(8,128)(2,1)S(1)} %get-tuple-element.36.refs_1_, bf16[512,256]{1,0:T(8,128)(2,1)S(1)} %collective-permute-done.11.refs_2_, bf16[512,256]{1,0:T(8,128)(2,1)S(1)} %collective-permute-done.12.refs_3_, ...), custom_call_target="tpu_custom_call" | custom-call | flops 268435456 | bytes 1196032 | tf_op jit(solution)/shard_map/pallas_call | solution.py:28
  39.5 1.6 %shard_map.120.refs_5_ = f32[256,128]{1,0:T(8,128)S(1)} custom-call(bf16[288,256]{1,0:T(8,128)(2,1)S(1)} %collective-permute-done.9.refs_0_, bf16[512,256]{1,0:T(8,128)(2,1)S(1)} %get-tuple-element.36.refs_1_, bf16[512,256]{1,0:T(8,128)(2,1)S(1)} %collective-permute-done.11.refs_2_, bf16[512,256]{1,0:T(8,128)(2,1)S(1)} %collective-permute-done.12.refs_3_, ...), custom_call_target="tpu_custom_call" | custom-call | flops 268435456 | bytes 1327104 | tf_op jit(solution)/shard_map/pallas_call | solution.py:28
  41.1 0.0 collective-permute-done.14.refs_0_
  41.1 1.6 %shard_map.121.refs_5_ = f32[256,128]{1,0:T(8,128)S(1)} custom-call(bf16[288,256]{1,0:T(8,128)(2,1)S(1)} %collective-permute-done.14.refs_0_, bf16[512,256]{1,0:T(8,128)(2,1)S(1)} %get-tuple-element.36.refs_1_, bf16[512,256]{1,0:T(8,128)(2,1)S(1)} %collective-permute-done.11.refs_2_, bf16[512,256]{1,0:T(8,128)(2,1)S(1)} %collective-permute-done.12.refs_3_, ...), custom_call_target="tpu_custom_call" | custom-call | flops 268435456 | bytes 1327104 | tf_op jit(solution)/shard_map/pallas_call | solution.py:28
  42.7 0.9 %collective-permute-done.10.refs_0_ = bf16[288,256]{1,0:T(8,128)(2,1)S(1)} collective-permute-done((bf16[288,256]{1,0:T(8,128)(2,1)S(1)}, bf16[288,256]{1,0:T(8,128)(2,1)S(1)}, u32[]{:S(2)}, u32[]{:S(2)}) %collective-permute-start.10) | collective-permute-done | bytes 147488 | tf_op jit(solution)/shard_map/ppermute | solution.py:52
  43.6 1.6 %shard_map.122.total_ref = f32[256,128]{1,0:T(8,128)S(1)} custom-call(bf16[288,256]{1,0:T(8,128)(2,1)S(1)} %collective-permute-done.10.refs_0_, bf16[512,256]{1,0:T(8,128)(2,1)S(1)} %get-tuple-element.36.refs_1_, bf16[512,256]{1,0:T(8,128)(2,1)S(1)} %collective-permute-done.11.refs_2_, bf16[512,256]{1,0:T(8,128)(2,1)S(1)} %collective-permute-done.12.refs_3_, ...), custom_call_target="tpu_custom_call" | custom-call | flops 268435456 | bytes 1327104 | tf_op jit(solution)/shard_map/pallas_call | solution.py:28
  45.1 0.2 shard_map.123
  45.3 11.5 %all_to_all.5.part_ref = f32[16,8,128]{2,1,0:T(8,128)S(1)} all-to-all(f32[16,8,128]{2,1,0:T(8,128)S(1)} %shard_map.123), channel_id=1, replica_groups=mesh['groups'=2,'blk'=16] {'blk'}, dimensions={0} | all-to-all | bytes 131072 | tf_op jit(solution)/shard_map/all_to_all | solution.py:420
  56.8 0.0 copy-done
  56.8 0.7 %shard_map.124 = f32[16,64]{1,0:T(8,128)} custom-call(f32[16,8,128]{2,1,0:T(8,128)S(1)} %all_to_all.5.part_ref, s32[1,64]{1,0:T(1,128)S(1)} %bitcast.5), custom_call_target="tpu_custom_call" | custom-call | bytes 65792 | tf_op jit(solution)/shard_map/pallas_call | solution.py:28
Async XLA Ops:
  0.6 4.9 %copy-start.3 = (bf16[1024,1024]{1,0:T(8,128)(2,1)S(1)}, bf16[1024,1024]{1,0:T(8,128)(2,1)}, u32[]{:S(2)}) copy-start(bf16[1024,1024]{1,0:T(8,128)(2,1)} %weight_ref.1) | copy-start | bytes 6291460
  0.6 1.1 %copy-start.5 = (bf16[64,2,1024]{2,1,0:T(2,128)(2,1)S(1)}, bf16[64,2,1024]{2,1,0:T(2,128)(2,1)}, u32[]{:S(2)}) copy-start(bf16[64,2,1024]{2,1,0:T(2,128)(2,1)} %kv_ref.1) | copy-start | bytes 786436
  1.7 3.8 %copy-start.6 = (bf16[64,1024]{1,0:T(8,128)(2,1)S(1)}, bf16[64,1024]{1,0:T(8,128)(2,1)}, u32[]{:S(2)}) copy-start(bf16[64,1024]{1,0:T(8,128)(2,1)} %event_ref.1) | copy-start | bytes 393220
  1.7 3.8 %copy-start.7 = (s32[8192]{0:T(1024)S(1)}, s32[8192]{0:T(1024)}, u32[]{:S(2)}) copy-start(s32[8192]{0:T(1024)} %param.11) | copy-start | bytes 98308
  1.7 3.8 %copy-start.8 = (s32[64,16]{0,1:T(8,128)S(1)}, s32[64,16]{0,1:T(8,128)}, u32[]{:S(2)}) copy-start(s32[64,16]{0,1:T(8,128)} %param.18) | copy-start | bytes 12292
  1.7 3.8 %copy-start.9 = (s32[64]{0:T(128)S(1)}, s32[64]{0:T(128)}, u32[]{:S(2)}) copy-start(s32[64]{0:T(128)} %param.17) | copy-start | bytes 772
  2.4 6.8 %collective-permute-start = (bf16[64,512]{1,0:T(8,128)(2,1)S(1)}, bf16[64,512]{1,0:T(8,128)(2,1)S(1)}, u32[]{:S(2)}, u32[]{:S(2)}) collective-permute-start(bf16[64,512]{1,0:T(8,128)(2,1)S(1)} %get-tuple-element.23), channel_id=1, source_target_pairs={{0,1},{1,0},{2,3},{3,2},{4,5},{5,4},{6,7},{7,6},{8,9},{9,8},{10,11... | collective-permute-start | bytes 196616 | tf_op jit(solution)/shard_map/ppermute | solution.py:42
  3.0 7.7 %collective-permute-start.1 = (bf16[64,512]{1,0:T(8,128)(2,1)S(1)}, bf16[64,512]{1,0:T(8,128)(2,1)S(1)}, u32[]{:S(2)}, u32[]{:S(2)}) collective-permute-start(bf16[64,512]{1,0:T(8,128)(2,1)S(1)} %get-tuple-element.24), channel_id=1, source_target_pairs={{0,2},{1,3},{2,0},{3,1},{4,6},{5,7},{6,4},{7,5},{8,10},{9,11},{10,... | collective-permute-start | bytes 196616 | tf_op jit(solution)/shard_map/ppermute | solution.py:42
  5.5 5.2 %collective-permute-start.2 = (bf16[64,512]{1,0:T(8,128)(2,1)S(1)}, bf16[64,512]{1,0:T(8,128)(2,1)S(1)}, u32[]{:S(2)}, u32[]{:S(2)}) collective-permute-start(bf16[64,512]{1,0:T(8,128)(2,1)S(1)} %get-tuple-element.25), channel_id=1, source_target_pairs={{0,3},{1,2},{2,1},{3,0},{4,7},{5,6},{6,5},{7,4},{8,11},{9,10},{10,... | collective-permute-start | bytes 196616 | tf_op jit(solution)/shard_map/ppermute | solution.py:42
  5.6 8.3 %copy-start.1 = (bf16[1024,2048]{1,0:T(8,128)(2,1)S(1)}, bf16[1024,2048]{1,0:T(8,128)(2,1)}, u32[]{:S(2)}) copy-start(bf16[1024,2048]{1,0:T(8,128)(2,1)} %up_ref.1) | copy-start | bytes 12582916
  5.6 8.3 %copy-start.2 = (bf16[2048,1024]{1,0:T(8,128)(2,1)S(1)}, bf16[2048,1024]{1,0:T(8,128)(2,1)}, u32[]{:S(2)}) copy-start(bf16[2048,1024]{1,0:T(8,128)(2,1)} %down_ref.1) | copy-start | bytes 12582916
  5.6 8.3 %copy-start.4 = (bf16[512,1024]{1,0:T(8,128)(2,1)S(1)}, bf16[512,1024]{1,0:T(8,128)(2,1)}, u32[]{:S(2)}) copy-start(bf16[512,1024]{1,0:T(8,128)(2,1)} %row_ref.1) | copy-start | bytes 3145732
  6.9 5.5 %collective-permute-start.4 = (bf16[80,256]{1,0:T(8,128)(2,1)S(1)}, bf16[80,256]{1,0:T(8,128)(2,1)S(1)}, u32[]{:S(2)}, u32[]{:S(2)}) collective-permute-start(bf16[80,256]{1,0:T(8,128)(2,1)S(1)} %get-tuple-element.28), channel_id=1, source_target_pairs={{0,1},{1,0},{2,3},{3,2},{4,5},{5,4},{6,7},{7,6},{8,9},{9,8},{10,11... | collective-permute-start | bytes 122888 | tf_op jit(solution)/shard_map/ppermute | solution.py:42
  7.2 13.7 %collective-permute-start.7 = (bf16[64,512]{1,0:T(8,128)(2,1)S(1)}, bf16[64,512]{1,0:T(8,128)(2,1)S(1)}, u32[]{:S(2)}, u32[]{:S(2)}) collective-permute-start(bf16[64,512]{1,0:T(8,128)(2,1)S(1)} %get-tuple-element.22.refs_0_.refs_4_), channel_id=1, source_target_pairs={{0,4},{1,5},{2,6},{3,7},{4,8},{5,9},{6,10},{7,11},{8,12},{9,13},{1... | collective-permute-start | bytes 196616 | tf_op jit(solution)/shard_map/ppermute | solution.py:47
  9.2 10.1 %collective-permute-start.5 = (bf16[80,256]{1,0:T(8,128)(2,1)S(1)}, bf16[80,256]{1,0:T(8,128)(2,1)S(1)}, u32[]{:S(2)}, u32[]{:S(2)}) collective-permute-start(bf16[80,256]{1,0:T(8,128)(2,1)S(1)} %get-tuple-element.29), channel_id=1, source_target_pairs={{0,2},{1,3},{2,0},{3,1},{4,6},{5,7},{6,4},{7,5},{8,10},{9,11},{10,... | collective-permute-start | bytes 122888 | tf_op jit(solution)/shard_map/ppermute | solution.py:42
  10.7 9.2 %collective-permute-start.6 = (bf16[80,256]{1,0:T(8,128)(2,1)S(1)}, bf16[80,256]{1,0:T(8,128)(2,1)S(1)}, u32[]{:S(2)}, u32[]{:S(2)}) collective-permute-start(bf16[80,256]{1,0:T(8,128)(2,1)S(1)} %get-tuple-element.30), channel_id=1, source_target_pairs={{0,3},{1,2},{2,1},{3,0},{4,7},{5,6},{6,5},{7,4},{8,11},{9,10},{10,... | collective-permute-start | bytes 122888 | tf_op jit(solution)/shard_map/ppermute | solution.py:42
  10.8 10.5 %collective-permute-start.8 = (bf16[192,512]{1,0:T(8,128)(2,1)S(1)}, bf16[192,512]{1,0:T(8,128)(2,1)S(1)}, u32[]{:S(2)}, u32[]{:S(2)}) collective-permute-start(bf16[192,512]{1,0:T(8,128)(2,1)S(1)} %get-tuple-element.31), channel_id=1, source_target_pairs={{0,4},{1,5},{2,6},{3,7},{4,8},{5,9},{6,10},{7,11},{8,12},{9,13},{1... | collective-permute-start | bytes 589832 | tf_op jit(solution)/shard_map/ppermute | solution.py:47
  12.4 16.1 %collective-permute-start.3 = (bf16[192,512]{1,0:T(8,128)(2,1)S(1)}, bf16[192,512]{1,0:T(8,128)(2,1)S(1)}, u32[]{:S(2)}, u32[]{:S(2)}) collective-permute-start(bf16[192,512]{1,0:T(8,128)(2,1)S(1)} %get-tuple-element.26), channel_id=1, source_target_pairs={{0,8},{1,9},{2,10},{3,11},{4,12},{5,13},{6,14},{7,15},{8,0},{9,1},... | collective-permute-start | bytes 589832 | tf_op jit(solution)/shard_map/ppermute | solution.py:47
  19.3 37.5 %copy-start = (s32[64]{0:T(128)S(1)}, s32[64]{0:T(128)}, u32[]{:S(2)}) copy-start(s32[64]{0:T(128)} %param.19) | copy-start | bytes 772
  19.3 18.5 %collective-permute-start.11 = (bf16[512,256]{1,0:T(8,128)(2,1)S(1)}, bf16[512,256]{1,0:T(8,128)(2,1)S(1)}, u32[]{:S(2)}, u32[]{:S(2)}) collective-permute-start(bf16[512,256]{1,0:T(8,128)(2,1)S(1)} %get-tuple-element.37), channel_id=1, source_target_pairs={{0,1},{1,0},{2,3},{3,2},{4,5},{5,4},{6,7},{7,6},{8,9},{9,8},{10,11... | collective-permute-start | bytes 786440 | tf_op jit(solution)/shard_map/ppermute | solution.py:42
  19.9 18.0 %collective-permute-start.12 = (bf16[512,256]{1,0:T(8,128)(2,1)S(1)}, bf16[512,256]{1,0:T(8,128)(2,1)S(1)}, u32[]{:S(2)}, u32[]{:S(2)}) collective-permute-start(bf16[512,256]{1,0:T(8,128)(2,1)S(1)} %get-tuple-element.38), channel_id=1, source_target_pairs={{0,2},{1,3},{2,0},{3,1},{4,6},{5,7},{6,4},{7,5},{8,10},{9,11},{10,... | collective-permute-start | bytes 786440 | tf_op jit(solution)/shard_map/ppermute | solution.py:42
  20.9 17.0 %collective-permute-start.13 = (bf16[512,256]{1,0:T(8,128)(2,1)S(1)}, bf16[512,256]{1,0:T(8,128)(2,1)S(1)}, u32[]{:S(2)}, u32[]{:S(2)}) collective-permute-start(bf16[512,256]{1,0:T(8,128)(2,1)S(1)} %get-tuple-element.39), channel_id=1, source_target_pairs={{0,3},{1,2},{2,1},{3,0},{4,7},{5,6},{6,5},{7,4},{8,11},{9,10},{10,... | collective-permute-start | bytes 786440 | tf_op jit(solution)/shard_map/ppermute | solution.py:42
  29.0 8.8 %collective-permute-start.9 = (bf16[288,256]{1,0:T(8,128)(2,1)S(1)}, bf16[288,256]{1,0:T(8,128)(2,1)S(1)}, u32[]{:S(2)}, u32[]{:S(2)}) collective-permute-start(bf16[288,256]{1,0:T(8,128)(2,1)S(1)} %shard_map.118.refs_0_), channel_id=1, source_target_pairs={{0,8},{1,9},{2,10},{3,11},{4,12},{5,13},{6,14},{7,15},{8,0},{9,1},... | collective-permute-start | bytes 442376 | tf_op jit(solution)/shard_map/ppermute | solution.py:52
  29.1 11.9 %collective-permute-start.14 = (bf16[288,256]{1,0:T(8,128)(2,1)S(1)}, bf16[288,256]{1,0:T(8,128)(2,1)S(1)}, u32[]{:S(2)}, u32[]{:S(2)}) collective-permute-start(bf16[288,256]{1,0:T(8,128)(2,1)S(1)} %shard_map.118.refs_0_), channel_id=1, source_target_pairs={{0,4},{1,5},{2,6},{3,7},{4,0},{5,1},{6,2},{7,3},{8,12},{9,13},{10,... | collective-permute-start | bytes 442376 | tf_op jit(solution)/shard_map/ppermute | solution.py:52
  37.8 5.7 %collective-permute-start.10 = (bf16[288,256]{1,0:T(8,128)(2,1)S(1)}, bf16[288,256]{1,0:T(8,128)(2,1)S(1)}, u32[]{:S(2)}, u32[]{:S(2)}) collective-permute-start(bf16[288,256]{1,0:T(8,128)(2,1)S(1)} %collective-permute-done.9.refs_0_), channel_id=1, source_target_pairs={{0,4},{1,5},{2,6},{3,7},{4,0},{5,1},{6,2},{7,3},{8,12},{9,13},{10,... | collective-permute-start | bytes 442376 | tf_op jit(solution)/shard_map/ppermute | solution.py:52

commit v2 on v1

--- a/solution.py
+++ b/solution.py
@@ -114,25 +114,46 @@
         query_outs[step][hist_rows:, :] = meta
 
 
+def late_blocks(column):
+    early = jnp.maximum(column, 1)
+    return early, jnp.where(early == 1, 2, 1), jnp.where(early == PLANE - 1, 2, PLANE - 1)
+
+
+def early_kernel(own_ref, near_ref, out_ref):
+    column = my_place()[1]
+
+    @pl.when(column == 0)
+    def _():
+        out_ref[...] = near_ref[...]
+
+    @pl.when(column > 0)
+    def _():
+        out_ref[...] = own_ref[...]
+
+
 def join_kernel(*refs):
     pieces, (rest_ref, late_ref) = refs[:PLANE], refs[PLANE:]
     column = my_place()[1]
     rows = pieces[0].shape[0]
     for step in range(1, PLANE):
         rest_ref[(step - 1) * rows : step * rows, :] = pieces[step][...]
-    for block in range(1, PLANE):
-        for step in range(PLANE):
+    for at, block in enumerate(late_blocks(column)[1:]):
+        for step in range(1, PLANE):
 
             @pl.when((column ^ block) == step)
-            def _(block=block, step=step):
-                late_ref[(block - 1) * rows : block * rows, :] = pieces[step][...]
+            def _(at=at, step=step):
+                late_ref[at * rows : (at + 1) * rows, :] = pieces[step][...]
 
 
 def key_positions(hist_rows, count, shift):
     plane, column = my_place()
     at = lax.broadcasted_iota(jnp.int32, (1, count), 1)
     block = at // hist_rows
-    block = (column ^ block) if count == PLANE * hist_rows else 1 + block
+    if count == PLANE * hist_rows:
+        block = column ^ block
+    else:
+        first, second, third = late_blocks(column)
+        block = jnp.where(block == 0, first, jnp.where(block == 1, second, third))
     return ((plane - shift) * PLANE + block) * hist_rows + at % hist_rows
 
 
@@ -189,19 +210,23 @@
 
 
 def far_kernel(
-    hist_rows, shift, key_ref, before_ref, query_ref, offset_ref, meta_ref, out_ref, total_ref
+    hist_rows,
+    shift,
+    early_ref,
+    late_ref,
+    before_ref,
+    query_ref,
+    offset_ref,
+    meta_ref,
+    out_ref,
+    total_ref,
 ):
     rows = total_ref.shape[0]
     total_ref[...] = before_ref[...]
-    key_pos = key_positions(hist_rows, key_ref.shape[0], shift)
-    add_attention(
-        total_ref,
-        query_ref[...],
-        query_positions(hist_rows),
-        offset_ref[:, :1],
-        key_ref[...],
-        key_pos,
-    )
+    keys = jnp.concatenate([early_ref[...], late_ref[...]], axis=0)
+    key_pos = key_positions(hist_rows, keys.shape[0], shift)
+    query_pos = query_positions(hist_rows)
+    add_attention(total_ref, query_ref[...], query_pos, offset_ref[:, :1], keys, key_pos)
     out_ref[:rows, :] = total_ref[...].astype(jnp.bfloat16)
     out_ref[rows:, :] = meta_ref[...]
 
@@ -343,13 +368,19 @@
         flops=COVER,
     )
     query_plane = [query_own[0]] + [in_plane(query_own[step], step) for step in steps]
+    kv_early = call(early_kernel, jax.ShapeDtypeStruct((hist_rows, 2 * part), bf16), kv_plane[:2])
     kv_rest, kv_late = call(
-        join_kernel, [jax.ShapeDtypeStruct((rows - hist_rows, 2 * part), bf16)] * 2, kv_plane
+        join_kernel,
+        [
+            jax.ShapeDtypeStruct((rows - hist_rows, 2 * part), bf16),
+            jax.ShapeDtypeStruct((rows - 2 * hist_rows, 2 * part), bf16),
+        ],
+        kv_plane,
     )
     kv_near = list(kv_plane)
     for shift in range(1, shifts):
         kv_near += [forward(kv_plane[0], shift), forward(kv_rest, shift)]
-    kv_far = forward(kv_late, shifts)
+    kv_far = [forward(kv_early, shifts), forward(kv_late, shifts)]
 
     mlp = call(
         mlp_kernel,
@@ -380,7 +411,7 @@
     user = call(
         functools.partial(far_kernel, hist_rows, shifts),
         jax.ShapeDtypeStruct((rows + near[3].shape[0], part), bf16),
-        [kv_far, *near],
+        [*kv_far, *near],
         [pltpu.VMEM((rows, part), jnp.float32)],
         flops=4 * rows * rows * part,
     )

time: 57.7 us -> 57.7 us (level)
  starting transfers between devices: 14.3 us -> 15.8 us
  waiting for transfers between devices: 13.7 us -> 12.2 us
    ppermute x3 -> x4, waiting for transfers between devices: 6.3 us -> 4.83 us  [forward(): lax.ppermute(value, 'blk', [(s, (s + step * PLANE) % count) for s in rang...]
    ppermute x3 -> x4, starting transfers between devices: 5.11 us -> 6.2 us  [forward(): lax.ppermute(value, 'blk', [(s, (s + step * PLANE) % count) for s in rang...]
    pallas_call x12 -> x13, Pallas kernels: 16.1 us -> 16 us  [call(): pl.pallas_call(body, out_shape=out_shape, in_specs=[VMEM_SPEC] * len(args...]
  transfers between devices with their start and end apart: 15 -> 16, of which waited for: 3 -> 3; matrix products, arithmetic and copies ran while one was open for 0% -> 0% of each run, Pallas kernels for 23% -> 23%
where the time goes in v2:
time: 57.7 us; the launch traced here: 57.5 us
  Pallas kernels  16 us (28%)
  starting transfers between devices  15.8 us (27%)
  waiting for transfers between devices  12.2 us (21%)
  blocking collectives  11.5 us (20%)
  local copies, waits for them, and re-layouts  1.14 us (2%)
  between operations  0.83 us (1%)
    pallas_call x13, Pallas kernels, call(): pl.pallas_call(body, out_shape=out_shape, in_specs=[VMEM_SPEC] * len(args...  16 us
    all_to_all x1, blocking collectives, per_device(): lax.all_to_all(partial, 'blk', split_axis=0, concat_axis=0, tiled=True)  11.5 us
    ppermute x3, waiting for transfers between devices, swap(): lax.ppermute(value, 'blk', [(s, s ^ step * PLANE) for s in range(count)])  7.36 us
    ppermute x9, starting transfers between devices, in_plane(): return lax.ppermute(value, 'blk', pairs)  7.26 us
    ppermute x4, starting transfers between devices, forward(): lax.ppermute(value, 'blk', [(s, (s + step * PLANE) % count) for s in rang...  6.2 us
    ppermute x4, waiting for transfers between devices, forward(): lax.ppermute(value, 'blk', [(s, (s + step * PLANE) % count) for s in rang...  4.83 us
    ppermute x3, starting transfers between devices, swap(): lax.ppermute(value, 'blk', [(s, s ^ step * PLANE) for s in range(count)])  2.31 us
  transfers between devices with their start and end apart: 16, of which 3 were waited for; matrix products, arithmetic and copies ran while one was open for 0% of the time, Pallas kernels for 23%

profile of v2, /device:TPU:0, one launch (start us, length us, event | category | flops | bytes accessed | tf_op | source)
XLA Modules:
  0.0 57.5 jit_solution(4336051267274596578)
XLA Ops:
  0.6 0.0 copy-start.3
  0.6 0.0 copy-start.5
  0.7 1.1 %copy-done.5 = bf16[64,2,1024]{2,1,0:T(2,128)(2,1)S(1)} copy-done((bf16[64,2,1024]{2,1,0:T(2,128)(2,1)S(1)}, bf16[64,2,1024]{2,1,0:T(2,128)(2,1)}, u32[]{:S(2)}) %copy-start.5) | copy-done | bytes 262168
  1.7 0.0 copy-start.6
  1.7 0.0 copy-start.7
  1.7 0.0 copy-start.8
  1.7 0.0 copy-start.9
  1.8 0.6 %shard_map.114 = (bf16[64,512]{1,0:T(8,128)(2,1)S(1)}, bf16[64,512]{1,0:T(8,128)(2,1)S(1)}, bf16[64,512]{1,0:T(8,128)(2,1)S(1)}, bf16[64,512]{1,0:T(8,128)(2,1)S(1)}) custom-call(bf16[64,2,1024]{2,1,0:T(2,128)(2,1)S(1)} %copy-done.5), custom_call_target="tpu_custom_call" | custom-call | flops 6000000000 | bytes 262144 | tf_op jit(solution)/shard_map/pallas_call | solution.py:28
  2.4 0.6 collective-permute-start
  3.0 2.6 %collective-permute-start.2 = (bf16[64,512]{1,0:T(8,128)(2,1)S(1)}, bf16[64,512]{1,0:T(8,128)(2,1)S(1)}, u32[]{:S(2)}, u32[]{:S(2)}) collective-permute-start(bf16[64,512]{1,0:T(8,128)(2,1)S(1)} %get-tuple-element.24), channel_id=1, source_target_pairs={{0,2},{1,3},{2,0},{3,1},{4,6},{5,7},{6,4},{7,5},{8,10},{9,11},{10,... | collective-permute-start | bytes 196616 | tf_op jit(solution)/shard_map/ppermute | solution.py:42
  5.5 0.0 collective-permute-start.3
  5.6 0.0 copy-done.3
  5.6 0.0 copy-done.6
  5.6 0.0 copy-done.7
  5.6 0.0 copy-done.8
  5.6 0.0 copy-done.9
  5.6 0.0 copy-start.1
  5.6 0.0 copy-start.2
  5.6 0.0 copy-start.4
  5.6 1.3 %shard_map.117 = (bf16[80,256]{1,0:T(8,128)(2,1)S(1)}, bf16[80,256]{1,0:T(8,128)(2,1)S(1)}, bf16[80,256]{1,0:T(8,128)(2,1)S(1)}, bf16[80,256]{1,0:T(8,128)(2,1)S(1)}) custom-call(bf16[64,1024]{1,0:T(8,128)(2,1)S(1)} %copy-done.6, bf16[1024,1024]{1,0:T(8,128)(2,1)S(1)} %copy-done.3, s32[16,64]{1,0:T(8,128)S(1)} %bitcast.7, s32[64,128]{1,0:T(8,128)S(1)} %bitcast.6, ...), custom_call_target="tpu_custom_call" | custom-call | flops 6000000000 | bytes 2265344 | tf_op jit(solution)/shard_map/pallas_call | solution.py:28
  6.9 0.2 collective-permute-start.5
  7.2 1.9 %collective-permute-start.6 = (bf16[80,256]{1,0:T(8,128)(2,1)S(1)}, bf16[80,256]{1,0:T(8,128)(2,1)S(1)}, u32[]{:S(2)}, u32[]{:S(2)}) collective-permute-start(bf16[80,256]{1,0:T(8,128)(2,1)S(1)} %get-tuple-element.29), channel_id=1, source_target_pairs={{0,2},{1,3},{2,0},{3,1},{4,6},{5,7},{6,4},{7,5},{8,10},{9,11},{10,... | collective-permute-start | bytes 122888 | tf_op jit(solution)/shard_map/ppermute | solution.py:42
  9.1 0.0 collective-permute-done.near_ref.refs_1_.refs_5_
  9.1 1.6 %collective-permute-start.8 = (bf16[64,512]{1,0:T(8,128)(2,1)S(1)}, bf16[64,512]{1,0:T(8,128)(2,1)S(1)}, u32[]{:S(2)}, u32[]{:S(2)}) collective-permute-start(bf16[64,512]{1,0:T(8,128)(2,1)S(1)} %get-tuple-element.22.own_ref.refs_0_.refs_4_), channel_id=1, source_target_pairs={{0,4},{1,5},{2,6},{3,7},{4,8},{5,9},{6,10},{7,11},{8,12},{9,13},{1... | collective-permute-start | bytes 196616 | tf_op jit(solution)/shard_map/ppermute | solution.py:47
  10.7 0.0 collective-permute-done.2.refs_2_.refs_6_
  10.7 0.0 collective-permute-start.7
  10.7 0.0 collective-permute-done.3.refs_3_.refs_7_
  10.8 1.6 %collective-permute-start.9 = (bf16[192,512]{1,0:T(8,128)(2,1)S(1)}, bf16[192,512]{1,0:T(8,128)(2,1)S(1)}, u32[]{:S(2)}, u32[]{:S(2)}) collective-permute-start(bf16[192,512]{1,0:T(8,128)(2,1)S(1)} %get-tuple-element.31), channel_id=1, source_target_pairs={{0,4},{1,5},{2,6},{3,7},{4,8},{5,9},{6,10},{7,11},{8,12},{9,13},{1... | collective-permute-start | bytes 589832 | tf_op jit(solution)/shard_map/ppermute | solution.py:47
  12.4 0.0 collective-permute-done.5.refs_1_
  12.4 1.5 %collective-permute-start.4 = (bf16[128,512]{1,0:T(8,128)(2,1)S(1)}, bf16[128,512]{1,0:T(8,128)(2,1)S(1)}, u32[]{:S(2)}, u32[]{:S(2)}) collective-permute-start(bf16[128,512]{1,0:T(8,128)(2,1)S(1)} %get-tuple-element.26), channel_id=1, source_target_pairs={{0,8},{1,9},{2,10},{3,11},{4,12},{5,13},{6,14},{7,15},{8,0},{9,1},... | collective-permute-start | bytes 393224 | tf_op jit(solution)/shard_map/ppermute | solution.py:47
  13.9 0.0 collective-permute-done.6.refs_2_
  13.9 1.4 %collective-permute-start.1 = (bf16[64,512]{1,0:T(8,128)(2,1)S(1)}, bf16[64,512]{1,0:T(8,128)(2,1)S(1)}, u32[]{:S(2)}, u32[]{:S(2)}) collective-permute-start(bf16[64,512]{1,0:T(8,128)(2,1)S(1)} %shard_map.115), channel_id=1, source_target_pairs={{0,8},{1,9},{2,10},{3,11},{4,12},{5,13},{6,14},{7,15},{8,0},{9,1},... | collective-permute-start | bytes 196616 | tf_op jit(solution)/shard_map/ppermute | solution.py:47
  15.4 0.0 copy-done.1
  15.4 0.0 copy-done.2
  15.4 0.0 copy-done.4
  15.4 5.4 %shard_map.113 = (bf16[512,1024]{1,0:T(8,128)(2,1)}, bf16[512,256]{1,0:T(8,128)(2,1)S(1)}, bf16[512,256]{1,0:T(8,128)(2,1)S(1)}, bf16[512,256]{1,0:T(8,128)(2,1)S(1)}, bf16[512,256]{1,0:T(8,128)(2,1)S(1)}) custom-call(bf16[512,1024]{1,0:T(8,128)(2,1)S(1)} %copy-done.4, bf16[1024,2048]{1,0:T(8,128)(2,1)S(1)} %copy-done.1, bf16[2048,1024]{1,0:T(8,128)(2,1)S(1)} %copy-done.2), custom_call_target="tpu_custom_call" | custom-call | flops 4294967296 | bytes 9437184 | tf_op jit(solution)/shard_map/pallas_call | solution.py:28
  20.8 0.0 copy-start
  20.8 0.0 collective-permute-done.7.refs_3_
  20.8 0.1 collective-permute-start.12
  20.9 0.0 collective-permute-done.8.refs_8_
  20.9 1.3 %collective-permute-start.13 = (bf16[512,256]{1,0:T(8,128)(2,1)S(1)}, bf16[512,256]{1,0:T(8,128)(2,1)S(1)}, u32[]{:S(2)}, u32[]{:S(2)}) collective-permute-start(bf16[512,256]{1,0:T(8,128)(2,1)S(1)} %get-tuple-element.38), channel_id=1, source_target_pairs={{0,2},{1,3},{2,0},{3,1},{4,6},{5,7},{6,4},{7,5},{8,10},{9,11},{10,... | collective-permute-start | bytes 786440 | tf_op jit(solution)/shard_map/ppermute | solution.py:42
  22.2 0.0 collective-permute-done.9.refs_9_
  22.2 0.6 collective-permute-start.14
  22.8 0.9 %shard_map.118 = (f32[256,256]{1,0:T(8,128)S(1)}, bf16[256,256]{1,0:T(8,128)(2,1)S(1)}, s32[256,128]{1,0:T(8,128)S(1)}, bf16[32,256]{1,0:T(8,128)(2,1)S(1)}) custom-call(bf16[80,256]{1,0:T(8,128)(2,1)S(1)} %get-tuple-element.27.refs_0_, bf16[80,256]{1,0:T(8,128)(2,1)S(1)} %collective-permute-done.5.refs_1_, ...), custom_call_target="tpu_custom_call" | custom-call | flops 134217728 | bytes 688128 | tf_op jit(solution)/shard_map/pallas_call | solution.py:28
  23.6 4.8 %collective-permute-done.1.early_ref = bf16[64,512]{1,0:T(8,128)(2,1)S(1)} collective-permute-done((bf16[64,512]{1,0:T(8,128)(2,1)S(1)}, bf16[64,512]{1,0:T(8,128)(2,1)S(1)}, u32[]{:S(2)}, u32[]{:S(2)}) %collective-permute-start.1) | collective-permute-done | bytes 65568 | tf_op jit(solution)/shard_map/ppermute | solution.py:47
  28.5 0.0 collective-permute-done.4.late_ref
  28.5 0.6 shard_map.119.refs_0_
  29.0 0.1 collective-permute-start.10
  29.1 2.2 %collective-permute-start.15 = (bf16[288,256]{1,0:T(8,128)(2,1)S(1)}, bf16[288,256]{1,0:T(8,128)(2,1)S(1)}, u32[]{:S(2)}, u32[]{:S(2)}) collective-permute-start(bf16[288,256]{1,0:T(8,128)(2,1)S(1)} %shard_map.119.refs_0_), channel_id=1, source_target_pairs={{0,4},{1,5},{2,6},{3,7},{4,0},{5,1},{6,2},{7,3},{8,12},{9,13},{10,... | collective-permute-start | bytes 442376 | tf_op jit(solution)/shard_map/ppermute | solution.py:52
  31.3 6.5 %collective-permute-done.10.refs_0_ = bf16[288,256]{1,0:T(8,128)(2,1)S(1)} collective-permute-done((bf16[288,256]{1,0:T(8,128)(2,1)S(1)}, bf16[288,256]{1,0:T(8,128)(2,1)S(1)}, u32[]{:S(2)}, u32[]{:S(2)}) %collective-permute-start.10) | collective-permute-done | bytes 147488 | tf_op jit(solution)/shard_map/ppermute | solution.py:52
  37.8 0.0 collective-permute-start.11
  37.8 0.0 collective-permute-done.12.refs_2_
  37.8 0.0 collective-permute-done.13.refs_3_
  37.8 0.0 collective-permute-done.14.refs_4_
  37.8 1.6 %shard_map.120.refs_5_ = f32[256,128]{1,0:T(8,128)S(1)} custom-call(bf16[288,256]{1,0:T(8,128)(2,1)S(1)} %shard_map.119.refs_0_, bf16[512,256]{1,0:T(8,128)(2,1)S(1)} %get-tuple-element.36.refs_1_, bf16[512,256]{1,0:T(8,128)(2,1)S(1)} %collective-permute-done.12.refs_2_, bf16[512,256]{1,0:T(8,128)(2,1)S(1)} %collective-permute-done.13.refs_3_, ...), custom_call_target="tpu_custom_call" | custom-call | flops 268435456 | bytes 1196032 | tf_op jit(solution)/shard_map/pallas_call | solution.py:28
  39.4 1.6 %shard_map.121.refs_5_ = f32[256,128]{1,0:T(8,128)S(1)} custom-call(bf16[288,256]{1,0:T(8,128)(2,1)S(1)} %collective-permute-done.10.refs_0_, bf16[512,256]{1,0:T(8,128)(2,1)S(1)} %get-tuple-element.36.refs_1_, bf16[512,256]{1,0:T(8,128)(2,1)S(1)} %collective-permute-done.12.refs_2_, bf16[512,256]{1,0:T(8,128)(2,1)S(1)} %collective-permute-done.13.refs_3_, ...), custom_call_target="tpu_custom_call" | custom-call | flops 268435456 | bytes 1327104 | tf_op jit(solution)/shard_map/pallas_call | solution.py:28
  41.0 0.0 collective-permute-done.15.refs_0_
  41.0 1.6 %shard_map.122.refs_5_ = f32[256,128]{1,0:T(8,128)S(1)} custom-call(bf16[288,256]{1,0:T(8,128)(2,1)S(1)} %collective-permute-done.15.refs_0_, bf16[512,256]{1,0:T(8,128)(2,1)S(1)} %get-tuple-element.36.refs_1_, bf16[512,256]{1,0:T(8,128)(2,1)S(1)} %collective-permute-done.12.refs_2_, bf16[512,256]{1,0:T(8,128)(2,1)S(1)} %collective-permute-done.13.refs_3_, ...), custom_call_target="tpu_custom_call" | custom-call | flops 268435456 | bytes 1327104 | tf_op jit(solution)/shard_map/pallas_call | solution.py:28
  42.6 0.9 %collective-permute-done.11.refs_0_ = bf16[288,256]{1,0:T(8,128)(2,1)S(1)} collective-permute-done((bf16[288,256]{1,0:T(8,128)(2,1)S(1)}, bf16[288,256]{1,0:T(8,128)(2,1)S(1)}, u32[]{:S(2)}, u32[]{:S(2)}) %collective-permute-start.11) | collective-permute-done | bytes 147488 | tf_op jit(solution)/shard_map/ppermute | solution.py:52
  43.5 1.6 %shard_map.123.total_ref = f32[256,128]{1,0:T(8,128)S(1)} custom-call(bf16[288,256]{1,0:T(8,128)(2,1)S(1)} %collective-permute-done.11.refs_0_, bf16[512,256]{1,0:T(8,128)(2,1)S(1)} %get-tuple-element.36.refs_1_, bf16[512,256]{1,0:T(8,128)(2,1)S(1)} %collective-permute-done.12.refs_2_, bf16[512,256]{1,0:T(8,128)(2,1)S(1)} %collective-permute-done.13.refs_3_, ...), custom_call_target="tpu_custom_call" | custom-call | flops 268435456 | bytes 1327104 | tf_op jit(solution)/shard_map/pallas_call | solution.py:28
  45.1 0.2 shard_map.124
  45.3 11.5 %all_to_all.5.part_ref = f32[16,8,128]{2,1,0:T(8,128)S(1)} all-to-all(f32[16,8,128]{2,1,0:T(8,128)S(1)} %shard_map.124), channel_id=1, replica_groups=mesh['groups'=2,'blk'=16] {'blk'}, dimensions={0} | all-to-all | bytes 131072 | tf_op jit(solution)/shard_map/all_to_all | solution.py:451
  56.8 0.0 copy-done
  56.8 0.7 %shard_map.125 = f32[16,64]{1,0:T(8,128)} custom-call(f32[16,8,128]{2,1,0:T(8,128)S(1)} %all_to_all.5.part_ref, s32[1,64]{1,0:T(1,128)S(1)} %bitcast.5), custom_call_target="tpu_custom_call" | custom-call | bytes 65792 | tf_op jit(solution)/shard_map/pallas_call | solution.py:28
  (2 shorter events, 0.1 us)
Async XLA Ops:
  0.6 4.9 %copy-start.3 = (bf16[1024,1024]{1,0:T(8,128)(2,1)S(1)}, bf16[1024,1024]{1,0:T(8,128)(2,1)}, u32[]{:S(2)}) copy-start(bf16[1024,1024]{1,0:T(8,128)(2,1)} %weight_ref.1) | copy-start | bytes 6291460
  0.6 1.1 %copy-start.5 = (bf16[64,2,1024]{2,1,0:T(2,128)(2,1)S(1)}, bf16[64,2,1024]{2,1,0:T(2,128)(2,1)}, u32[]{:S(2)}) copy-start(bf16[64,2,1024]{2,1,0:T(2,128)(2,1)} %kv_ref.1) | copy-start | bytes 786436
  1.7 3.8 %copy-start.6 = (bf16[64,1024]{1,0:T(8,128)(2,1)S(1)}, bf16[64,1024]{1,0:T(8,128)(2,1)}, u32[]{:S(2)}) copy-start(bf16[64,1024]{1,0:T(8,128)(2,1)} %event_ref.1) | copy-start | bytes 393220
  1.7 3.8 %copy-start.7 = (s32[8192]{0:T(1024)S(1)}, s32[8192]{0:T(1024)}, u32[]{:S(2)}) copy-start(s32[8192]{0:T(1024)} %param.11) | copy-start | bytes 98308
  1.7 3.8 %copy-start.8 = (s32[64,16]{0,1:T(8,128)S(1)}, s32[64,16]{0,1:T(8,128)}, u32[]{:S(2)}) copy-start(s32[64,16]{0,1:T(8,128)} %param.18) | copy-start | bytes 12292
  1.7 3.8 %copy-start.9 = (s32[64]{0:T(128)S(1)}, s32[64]{0:T(128)}, u32[]{:S(2)}) copy-start(s32[64]{0:T(128)} %param.17) | copy-start | bytes 772
  2.4 6.7 %collective-permute-start = (bf16[64,512]{1,0:T(8,128)(2,1)S(1)}, bf16[64,512]{1,0:T(8,128)(2,1)S(1)}, u32[]{:S(2)}, u32[]{:S(2)}) collective-permute-start(bf16[64,512]{1,0:T(8,128)(2,1)S(1)} %get-tuple-element.23), channel_id=1, source_target_pairs={{0,1},{1,0},{2,3},{3,2},{4,5},{5,4},{6,7},{7,6},{8,9},{9,8},{10,11... | collective-permute-start | bytes 196616 | tf_op jit(solution)/shard_map/ppermute | solution.py:42
  3.0 7.7 %collective-permute-start.2 = (bf16[64,512]{1,0:T(8,128)(2,1)S(1)}, bf16[64,512]{1,0:T(8,128)(2,1)S(1)}, u32[]{:S(2)}, u32[]{:S(2)}) collective-permute-start(bf16[64,512]{1,0:T(8,128)(2,1)S(1)} %get-tuple-element.24), channel_id=1, source_target_pairs={{0,2},{1,3},{2,0},{3,1},{4,6},{5,7},{6,4},{7,5},{8,10},{9,11},{10,... | collective-permute-start | bytes 196616 | tf_op jit(solution)/shard_map/ppermute | solution.py:42
  5.5 5.2 %collective-permute-start.3 = (bf16[64,512]{1,0:T(8,128)(2,1)S(1)}, bf16[64,512]{1,0:T(8,128)(2,1)S(1)}, u32[]{:S(2)}, u32[]{:S(2)}) collective-permute-start(bf16[64,512]{1,0:T(8,128)(2,1)S(1)} %get-tuple-element.25), channel_id=1, source_target_pairs={{0,3},{1,2},{2,1},{3,0},{4,7},{5,6},{6,5},{7,4},{8,11},{9,10},{10,... | collective-permute-start | bytes 196616 | tf_op jit(solution)/shard_map/ppermute | solution.py:42
  5.6 9.8 %copy-start.1 = (bf16[1024,2048]{1,0:T(8,128)(2,1)S(1)}, bf16[1024,2048]{1,0:T(8,128)(2,1)}, u32[]{:S(2)}) copy-start(bf16[1024,2048]{1,0:T(8,128)(2,1)} %up_ref.1) | copy-start | bytes 12582916
  5.6 9.8 %copy-start.2 = (bf16[2048,1024]{1,0:T(8,128)(2,1)S(1)}, bf16[2048,1024]{1,0:T(8,128)(2,1)}, u32[]{:S(2)}) copy-start(bf16[2048,1024]{1,0:T(8,128)(2,1)} %down_ref.1) | copy-start | bytes 12582916
  5.6 9.8 %copy-start.4 = (bf16[512,1024]{1,0:T(8,128)(2,1)S(1)}, bf16[512,1024]{1,0:T(8,128)(2,1)}, u32[]{:S(2)}) copy-start(bf16[512,1024]{1,0:T(8,128)(2,1)} %row_ref.1) | copy-start | bytes 3145732
  6.9 5.5 %collective-permute-start.5 = (bf16[80,256]{1,0:T(8,128)(2,1)S(1)}, bf16[80,256]{1,0:T(8,128)(2,1)S(1)}, u32[]{:S(2)}, u32[]{:S(2)}) collective-permute-start(bf16[80,256]{1,0:T(8,128)(2,1)S(1)} %get-tuple-element.28), channel_id=1, source_target_pairs={{0,1},{1,0},{2,3},{3,2},{4,5},{5,4},{6,7},{7,6},{8,9},{9,8},{10,11... | collective-permute-start | bytes 122888 | tf_op jit(solution)/shard_map/ppermute | solution.py:42
  7.2 6.8 %collective-permute-start.6 = (bf16[80,256]{1,0:T(8,128)(2,1)S(1)}, bf16[80,256]{1,0:T(8,128)(2,1)S(1)}, u32[]{:S(2)}, u32[]{:S(2)}) collective-permute-start(bf16[80,256]{1,0:T(8,128)(2,1)S(1)} %get-tuple-element.29), channel_id=1, source_target_pairs={{0,2},{1,3},{2,0},{3,1},{4,6},{5,7},{6,4},{7,5},{8,10},{9,11},{10,... | collective-permute-start | bytes 122888 | tf_op jit(solution)/shard_map/ppermute | solution.py:42
  9.1 11.8 %collective-permute-start.8 = (bf16[64,512]{1,0:T(8,128)(2,1)S(1)}, bf16[64,512]{1,0:T(8,128)(2,1)S(1)}, u32[]{:S(2)}, u32[]{:S(2)}) collective-permute-start(bf16[64,512]{1,0:T(8,128)(2,1)S(1)} %get-tuple-element.22.own_ref.refs_0_.refs_4_), channel_id=1, source_target_pairs={{0,4},{1,5},{2,6},{3,7},{4,8},{5,9},{6,10},{7,11},{8,12},{9,13},{1... | collective-permute-start | bytes 196616 | tf_op jit(solution)/shard_map/ppermute | solution.py:47
  10.7 10.1 %collective-permute-start.7 = (bf16[80,256]{1,0:T(8,128)(2,1)S(1)}, bf16[80,256]{1,0:T(8,128)(2,1)S(1)}, u32[]{:S(2)}, u32[]{:S(2)}) collective-permute-start(bf16[80,256]{1,0:T(8,128)(2,1)S(1)} %get-tuple-element.30), channel_id=1, source_target_pairs={{0,3},{1,2},{2,1},{3,0},{4,7},{5,6},{6,5},{7,4},{8,11},{9,10},{10,... | collective-permute-start | bytes 122888 | tf_op jit(solution)/shard_map/ppermute | solution.py:42
  10.8 11.4 %collective-permute-start.9 = (bf16[192,512]{1,0:T(8,128)(2,1)S(1)}, bf16[192,512]{1,0:T(8,128)(2,1)S(1)}, u32[]{:S(2)}, u32[]{:S(2)}) collective-permute-start(bf16[192,512]{1,0:T(8,128)(2,1)S(1)} %get-tuple-element.31), channel_id=1, source_target_pairs={{0,4},{1,5},{2,6},{3,7},{4,8},{5,9},{6,10},{7,11},{8,12},{9,13},{1... | collective-permute-start | bytes 589832 | tf_op jit(solution)/shard_map/ppermute | solution.py:47
  12.4 16.1 %collective-permute-start.4 = (bf16[128,512]{1,0:T(8,128)(2,1)S(1)}, bf16[128,512]{1,0:T(8,128)(2,1)S(1)}, u32[]{:S(2)}, u32[]{:S(2)}) collective-permute-start(bf16[128,512]{1,0:T(8,128)(2,1)S(1)} %get-tuple-element.26), channel_id=1, source_target_pairs={{0,8},{1,9},{2,10},{3,11},{4,12},{5,13},{6,14},{7,15},{8,0},{9,1},... | collective-permute-start | bytes 393224 | tf_op jit(solution)/shard_map/ppermute | solution.py:47
  13.9 14.5 %collective-permute-start.1 = (bf16[64,512]{1,0:T(8,128)(2,1)S(1)}, bf16[64,512]{1,0:T(8,128)(2,1)S(1)}, u32[]{:S(2)}, u32[]{:S(2)}) collective-permute-start(bf16[64,512]{1,0:T(8,128)(2,1)S(1)} %shard_map.115), channel_id=1, source_target_pairs={{0,8},{1,9},{2,10},{3,11},{4,12},{5,13},{6,14},{7,15},{8,0},{9,1},... | collective-permute-start | bytes 196616 | tf_op jit(solution)/shard_map/ppermute | solution.py:47
  20.8 36.0 %copy-start = (s32[64]{0:T(128)S(1)}, s32[64]{0:T(128)}, u32[]{:S(2)}) copy-start(s32[64]{0:T(128)} %param.19) | copy-start | bytes 772
  20.8 17.0 %collective-permute-start.12 = (bf16[512,256]{1,0:T(8,128)(2,1)S(1)}, bf16[512,256]{1,0:T(8,128)(2,1)S(1)}, u32[]{:S(2)}, u32[]{:S(2)}) collective-permute-start(bf16[512,256]{1,0:T(8,128)(2,1)S(1)} %get-tuple-element.37), channel_id=1, source_target_pairs={{0,1},{1,0},{2,3},{3,2},{4,5},{5,4},{6,7},{7,6},{8,9},{9,8},{10,11... | collective-permute-start | bytes 786440 | tf_op jit(solution)/shard_map/ppermute | solution.py:42
  20.9 16.9 %collective-permute-start.13 = (bf16[512,256]{1,0:T(8,128)(2,1)S(1)}, bf16[512,256]{1,0:T(8,128)(2,1)S(1)}, u32[]{:S(2)}, u32[]{:S(2)}) collective-permute-start(bf16[512,256]{1,0:T(8,128)(2,1)S(1)} %get-tuple-element.38), channel_id=1, source_target_pairs={{0,2},{1,3},{2,0},{3,1},{4,6},{5,7},{6,4},{7,5},{8,10},{9,11},{10,... | collective-permute-start | bytes 786440 | tf_op jit(solution)/shard_map/ppermute | solution.py:42
  22.2 15.6 %collective-permute-start.14 = (bf16[512,256]{1,0:T(8,128)(2,1)S(1)}, bf16[512,256]{1,0:T(8,128)(2,1)S(1)}, u32[]{:S(2)}, u32[]{:S(2)}) collective-permute-start(bf16[512,256]{1,0:T(8,128)(2,1)S(1)} %get-tuple-element.39), channel_id=1, source_target_pairs={{0,3},{1,2},{2,1},{3,0},{4,7},{5,6},{6,5},{7,4},{8,11},{9,10},{10,... | collective-permute-start | bytes 786440 | tf_op jit(solution)/shard_map/ppermute | solution.py:42
  29.0 8.8 %collective-permute-start.10 = (bf16[288,256]{1,0:T(8,128)(2,1)S(1)}, bf16[288,256]{1,0:T(8,128)(2,1)S(1)}, u32[]{:S(2)}, u32[]{:S(2)}) collective-permute-start(bf16[288,256]{1,0:T(8,128)(2,1)S(1)} %shard_map.119.refs_0_), channel_id=1, source_target_pairs={{0,8},{1,9},{2,10},{3,11},{4,12},{5,13},{6,14},{7,15},{8,0},{9,1},... | collective-permute-start | bytes 442376 | tf_op jit(solution)/shard_map/ppermute | solution.py:52
  29.1 11.9 %collective-permute-start.15 = (bf16[288,256]{1,0:T(8,128)(2,1)S(1)}, bf16[288,256]{1,0:T(8,128)(2,1)S(1)}, u32[]{:S(2)}, u32[]{:S(2)}) collective-permute-start(bf16[288,256]{1,0:T(8,128)(2,1)S(1)} %shard_map.119.refs_0_), channel_id=1, source_target_pairs={{0,4},{1,5},{2,6},{3,7},{4,0},{5,1},{6,2},{7,3},{8,12},{9,13},{10,... | collective-permute-start | bytes 442376 | tf_op jit(solution)/shard_map/ppermute | solution.py:52
  37.8 5.7 %collective-permute-start.11 = (bf16[288,256]{1,0:T(8,128)(2,1)S(1)}, bf16[288,256]{1,0:T(8,128)(2,1)S(1)}, u32[]{:S(2)}, u32[]{:S(2)}) collective-permute-start(bf16[288,256]{1,0:T(8,128)(2,1)S(1)} %collective-permute-done.10.refs_0_), channel_id=1, source_target_pairs={{0,4},{1,5},{2,6},{3,7},{4,0},{5,1},{6,2},{7,3},{8,12},{9,13},{10,... | collective-permute-start | bytes 442376 | tf_op jit(solution)/shard_map/ppermute | solution.py:52
